TPU v7x, 512 devices: a whole 4x8x8 slice. The times are simulated.
512 devices in a mesh: grp: 64 (over y, z), sta: 8 (over x, core).
Axes of the slice: x: 4, y: 8, z: 8, core: 2. Of those that a mesh axis runs over, the one named last changes fastest.
Arguments:
- seismograms: float32 [2048, 16, 4, 2063], P(('grp', 'sta')), may hold values from -6 to 6
- fir_taps: float32 [4, 16], replicated, may hold values from -0.75 to 0.75
- valid_windows: int32 [2048, 16], P('grp'), may hold values from 0 to 1, as said below
- pair_owners: int32 [64, 72, 1], P('grp'), may hold values from 0 to 63; in each aligned block of 72 rows (0 to 71, 72 to 143, ..., all dimensions but the last counted through in order) at most 2 rows name the same one
Outputs:
- correlations: float32 [64, 64, 2, 8, 2001], P('grp', None, None, 'sta')
Inputs may be any that keep to these rules, and one draw needn't show every extreme that they name: `pair_owners`: among the 72 pair blocks of one group, at most 2 have the same owner. `valid_windows`: some stations, at least one, have no usable window at all.
All inputs are finite; a program needn't handle non-finite values.
Results may differ from a plain program's by a relative error of at most 0.0027.
Values may be sent and summed in bfloat16 or wider, within the bound.
A program may use at most 64 MiB of HBM per device.

v0:
```python
import math

import jax
import jax.numpy as jnp
import numpy as np
from jax import lax
from jax.sharding import PartitionSpec as P

SEG = 2048
NB = 256
K0 = 16
SMOOTH = 32
MAXLAG = 1000
CAP = 2
SPLIT = 2


EPSILON = 1e-06
PRECISE = lax.Precision.HIGHEST


def decimate(raw_block, fir_taps):
    samples = raw_block.shape[-1] - fir_taps.shape[1] + 1
    filtered = jnp.zeros(raw_block.shape[:2] + (samples,), jnp.float32)
    for offset in range(fir_taps.shape[1]):
        segment_part = raw_block[:, :, :, offset : offset + samples]
        filtered = filtered + jnp.sum(
            segment_part * fir_taps[None, None, :, offset : offset + 1], axis=2
        )
    return filtered


def smoother():
    positions = jnp.arange(NB)
    nearby = jnp.abs(positions[:, None] - positions[None, :]) <= SMOOTH
    return nearby.astype(jnp.float32) / (2 * SMOOTH + 1)


def forward_table(samples):
    sample_ids = jnp.arange(samples, dtype=jnp.int32)[:, None]
    bin_ids = (K0 + jnp.arange(NB, dtype=jnp.int32))[None, :]
    turns = sample_ids * bin_ids % (2 * samples)
    radians = turns.astype(jnp.float32) * (math.pi / samples)
    return jnp.concatenate([jnp.cos(radians), -jnp.sin(radians)], axis=1)


def lag_table():
    bin_ids = (K0 + jnp.arange(NB, dtype=jnp.int32))[:, None]
    lag_ids = (jnp.arange(2 * MAXLAG + 1, dtype=jnp.int32) - MAXLAG)[None, :]
    turns = bin_ids * lag_ids % (2 * SEG)
    radians = turns.astype(jnp.float32) * (math.pi / SEG)
    return jnp.concatenate([jnp.cos(radians), -jnp.sin(radians)], axis=0)


def whiten(series, valid_rows):
    samples = series.shape[-1]
    spectrum_rows = series.reshape(-1, samples)
    spectrum = jnp.dot(
        spectrum_rows, forward_table(samples), precision=PRECISE, preferred_element_type=jnp.float32
    )
    real_part = spectrum[:, :NB]
    imag_part = spectrum[:, NB:]
    band_power = real_part * real_part + imag_part * imag_part
    smoothed = jnp.dot(
        band_power, smoother(), precision=PRECISE, preferred_element_type=jnp.float32
    )
    whitener = valid_rows.reshape(-1, 1).astype(jnp.float32) / jnp.sqrt(smoothed + EPSILON)
    whitened = spectrum * jnp.concatenate([whitener, whitener], axis=1)
    return whitened.reshape(series.shape[:2] + (2 * NB,)).astype(jnp.bfloat16)


def pair_stacks(left_side, right_side):
    left_re = left_side[..., :NB].astype(jnp.float32)
    left_im = left_side[..., NB:].astype(jnp.float32)
    right_re = right_side[..., :NB].astype(jnp.float32)
    right_im = right_side[..., NB:].astype(jnp.float32)
    real_sum = jnp.sum(left_re * right_re + left_im * right_im, axis=-2)
    imag_sum = jnp.sum(left_im * right_re - left_re * right_im, axis=-2)
    return jnp.concatenate([real_sum, imag_sum], axis=-1)


def placement_table(owner_ids, groups):
    block_count = owner_ids.shape[0]
    pair_ids = jnp.arange(block_count, dtype=jnp.int32)
    earlier = pair_ids[None, :] < pair_ids[:, None]
    same_owner = owner_ids[:, None] == owner_ids[None, :]
    slot_index = jnp.sum((earlier & same_owner).astype(jnp.int32), axis=1)
    hit_owner = owner_ids[None, None, :] == jnp.arange(groups, dtype=jnp.int32)[:, None, None]
    hit_slot = slot_index[None, None, :] == jnp.arange(CAP, dtype=jnp.int32)[None, :, None]
    return (hit_owner & hit_slot).astype(jnp.float32)


def route_stacks(placement, stacks):
    return jnp.einsum("ocp,pxf->ocxf", placement, stacks, precision=PRECISE)


def to_lags(received):
    summed, counts = received
    normalizer = 1.0 / (math.sqrt(NB) * jnp.maximum(counts, 1.0))
    flattened = (summed * normalizer[..., None]).reshape(-1, summed.shape[-1])
    lagged = jnp.dot(flattened, lag_table(), precision=PRECISE, preferred_element_type=jnp.float32)
    return lagged.reshape(summed.shape[:-1] + (lagged.shape[-1],))


def local(seismograms, fir_taps, valid_windows, pair_owners):
    stations = seismograms.shape[0]
    members = lax.axis_size("sta")
    groups = lax.axis_size("grp")
    member = lax.axis_index("sta")
    own_valid = lax.dynamic_slice_in_dim(valid_windows, member * stations, stations, 0)
    spectra = whiten(decimate(seismograms, fir_taps), own_valid)
    row_blocks, col_blocks = np.triu_indices(members)
    block_count = row_blocks.shape[0]
    pair_total = block_count * SPLIT
    left_rows = stations // SPLIT
    pair_width = left_rows * stations
    placement = placement_table(pair_owners[0, :, 0], groups)
    mask_blocks = valid_windows.astype(jnp.float32).reshape(members, stations, -1)
    pair_count = jnp.einsum(
        "paw,pbw->pab", mask_blocks[row_blocks], mask_blocks[col_blocks], precision=PRECISE
    ).reshape(pair_total, pair_width)
    count_buffer = jnp.einsum("ocp,px->ocx", placement, pair_count, precision=PRECISE)
    share = pair_width // members
    first_pair = member * share
    window_part = lax.all_to_all(spectra, "sta", split_axis=1, concat_axis=0, tiled=True)
    blocks = window_part.reshape(members, stations, window_part.shape[1], window_part.shape[2])
    left_side = blocks[row_blocks][:, :, None]
    right_side = blocks[col_blocks][:, None]
    stacks = pair_stacks(left_side, right_side).reshape(pair_total, pair_width, 2 * NB)
    partial_value = route_stacks(placement, stacks)
    arrived, arrived_counts = (
        lax.all_to_all(partial_value, "grp", split_axis=0, concat_axis=0, tiled=True),
        lax.all_to_all(count_buffer, "grp", split_axis=0, concat_axis=0, tiled=True),
    )
    summed = lax.psum_scatter(arrived, "sta", scatter_dimension=2, tiled=True)
    own_counts = lax.dynamic_slice_in_dim(arrived_counts, first_pair, share, 2)
    result = to_lags((summed, own_counts))
    return result[None]


def solution(mesh):
    in_specs = (P(("grp", "sta"), None, None, None), P(), P("grp", None), P("grp", None, None))
    out_specs = P("grp", None, None, "sta", None)
    return jax.shard_map(local, mesh=mesh, in_specs=in_specs, out_specs=out_specs, check_vma=False)
```

profile of v0, /device:TPU:1, one launch (start us, length us, event | category | flops | bytes accessed | tf_op | source)
XLA Modules:
  0.0 227.1 jit_solution(12501344924974740037)
XLA Ops:
  6.5 1.7 slice_reduce_fusion.14
  8.2 0.0 copy-start.3
  8.3 0.0 copy-start
  8.3 9.4 %fusion.22 = (f32[2048,256]{1,0:T(8,128)}, f32[2048,256]{1,0:T(8,128)}) fusion(s32[256]{0:T(256)S(1)} %iota_add_fusion.1), kind=kLoop, calls=%fused_computation.57 | loop fusion | flops 7864320 | bytes 4195328 | tf_op jit(solution)/shard_map/cos | solution.py:44
  17.6 0.1 copy.45
  17.7 0.1 convert_element_type.42
  17.8 11.8 %multiply_reduce_fusion.15 = (f32[4,16,2048]{2,1,0:T(8,128)S(1)}, f32[4,16,2048]{2,1,0:T(8,128)S(1)}, f32[4,16,2048]{2,1,0:T(8,128)S(1)}, f32[4,16,2048]{2,1,0:T...) fusion(f32[4,16,4,2063]{3,2,1,0:T(4,128)S(1)} %copy-done, ...), kind=kLoop, calls=%fused_computation.42 | loop fusion | flops 6422528 | bytes 18350192 | tf_op jit(solution)/shard_map/reduce_sum | solution.py:27
  29.6 14.9 %multiply_reduce_fusion.14 = (f32[4,16,2048]{2,1,0:T(8,128)S(1)}, f32[4,16,2048]{2,1,0:T(8,128)S(1)}, f32[4,16,2048]{2,1,0:T(8,128)S(1)}, f32[4,16,2048]{2,1,0:T...) fusion(f32[4,16,4,2063]{3,2,1,0:T(4,128)S(1)} %copy-done, ...), kind=kLoop, calls=%fused_computation.41 | loop fusion | flops 8257536 | bytes 23593104 | tf_op jit(solution)/shard_map/reduce_sum | solution.py:27
  44.6 0.7 add_add_fusion
  45.3 0.8 copy-done.1
  46.2 0.6 copy-done.2
  46.8 2.6 %fusion = f32[64,512]{1,0:T(8,128)S(1)} fusion(f32[64,2048]{1,0:T(8,128)S(1)} %bitcast.66, f32[2048,256]{1,0:T(8,128)S(1)} %copy-done.2, f32[2048,256]{1,0:T(8,128)S(1)} %copy-done.1), kind=kOutput, calls=%fused_computation.4 | convolution fusion | flops 806354944 | bytes 4849664 | tf_op jit(solution)/shard_map/dot_general | solution.py:58
  49.5 0.3 fusion.21
  49.8 0.7 copy.46
  50.4 10.1 %all-to-all-start = ((bf16[4,16,512]{2,0,1:T(4,128)(2,1)}), bf16[4,16,512]{2,0,1:T(4,128)(2,1)S(1)}, u32[]{:S(2)}, u32[]{:S(2)}) async-start(bf16[4,16,512]{2,0,1:T(4,128)(2,1)} %copy.46), calls=%async_computation | async-start | bytes 131072 | tf_op jit(solution)/shard_map/all_to_all | solution.py:125
  60.6 0.2 convert_reduce_fusion
  60.8 4.6 %all-to-all-done = bf16[4,16,512]{2,0,1:T(4,128)(2,1)S(1)} async-done(((bf16[4,16,512]{2,0,1:T(4,128)(2,1)}), bf16[4,16,512]{2,0,1:T(4,128)(2,1)S(1)}, u32[]{:S(2)}, u32[]{:S(2)}) %all-to-all-start) | async-done | bytes 65568 | tf_op jit(solution)/shard_map/all_to_all | solution.py:125
  65.4 0.8 gather_fusion
  66.2 0.1 fusion.30
  66.3 0.2 copy.47
  66.5 0.2 copy.48
  66.7 0.8 gather_fusion.1
  67.5 0.1 fusion.29
  67.6 1.2 add_reduce_fusion
  68.8 0.3 pad_maximum_fusion
  69.2 0.4 reshape.136
  69.6 1.7 fusion.17
  71.3 2.6 %copy.50 = f32[64,2,8,512]{3,2,1,0:T(8,128)} copy(f32[64,2,8,512]{3,0,2,1:T(8,128)S(1)} %fusion.17) | data formatting | bytes 4194304 | tf_op jit(solution)/shard_map/ocp,pxf->ocxf/dot_general | solution.py:94
  73.9 12.0 %all-to-all-start.1 = ((f32[64,2,8,512]{3,2,1,0:T(8,128)}), f32[64,2,8,512]{3,2,1,0:T(8,128)S(1)}, u32[]{:S(2)}, u32[]{:S(2)}) async-start(f32[64,2,8,512]{3,2,1,0:T(8,128)} %copy.50), calls=%async_computation.1 | async-start | bytes 4194304 | tf_op jit(solution)/shard_map/all_to_all | solution.py:132
  85.9 0.3 all-reduce.3.cloned.1.call-start
  86.1 0.6 gather_fusion.2
  86.8 0.6 gather_fusion.3
  87.4 0.4 fusion.52
  87.7 0.1 reshape.138
  87.8 46.9 %all-to-all-done.1 = f32[64,2,8,512]{3,2,1,0:T(8,128)S(1)} async-done(((f32[64,2,8,512]{3,2,1,0:T(8,128)}), f32[64,2,8,512]{3,2,1,0:T(8,128)S(1)}, u32[]{:S(2)}, u32[]{:S(2)}) %all-to-all-start.1) | async-done | bytes 2097184 | tf_op jit(solution)/shard_map/all_to_all | solution.py:132
  134.8 2.5 %copy.51 = f32[64,2,8,512]{3,0,2,1:T(8,128)} copy(f32[64,2,8,512]{3,2,1,0:T(8,128)S(1)} %all-to-all-done.1) | data formatting | bytes 4194304 | tf_op jit(solution)/shard_map/all_to_all | solution.py:132
  137.3 0.0 all-reduce.3.cloned.1.call-update
  137.3 0.2 fusion.36
  137.5 0.8 copy.54
  138.3 12.3 %all-to-all-start.2 = ((f32[64,2,8]{2,1,0:T(2,128)}), f32[64,2,8]{2,1,0:T(2,128)S(1)}, u32[]{:S(2)}, u32[]{:S(2)}) async-start(f32[64,2,8]{2,1,0:T(2,128)} %copy.54), calls=%async_computation.2 | async-start | bytes 131072 | tf_op jit(solution)/shard_map/all_to_all | solution.py:133
  150.6 9.5 %fusion.23 = (f32[256,2001]{0,1:T(8,128)S(1)}, f32[256,2001]{0,1:T(8,128)}) fusion(s32[2001]{0:T(1024)S(1)} %iota_add_fusion, s32[256]{0:T(256)S(1)} %iota_add_fusion.1), kind=kLoop, calls=%fused_computation.58 | loop fusion | flops 7683840 | bytes 4107076 | tf_op jit(solution)/shard_map/cos | solution.py:52
  160.2 1.3 dynamic-slice
  161.5 0.3 all-to-all-done.2
  161.8 0.1 constant_dynamic-slice_fusion
  161.9 0.1 copy.62
  162.0 50.1 %all-reduce.3.cloned.1.call-done = f32[64,2,8,512]{3,0,2,1:T(8,128)} async-done(((f32[64,2,8,512]{3,0,2,1:T(8,128)}), f32[64,2,8,512]{3,0,2,1:T(8,128)}) %all-reduce.3.cloned.1.call-update) | async-done | bytes 2097168
  212.1 6.2 %fusion.7 = f32[1,64,2,1,2001]{4,1,2,3,0:T(8,128)S(1)} fusion(f32[256,2001]{0,1:T(8,128)} %get-tuple-element.44, f32[256,2001]{0,1:T(8,128)S(1)} %get-tuple-element.43, f32[64,2,8,512]{3,0,2,1:T(8,128)} %all-reduce.3.cloned.1.call-done, u32[]{:T(128)} %bitcast.34, f32[64,2]{0,1:T(2,128)S(1)} %divide_bitcast_fusion), kind=kOutput, calls=%fused_computation.20 | convolution fusion | flops 1574740480 | bytes 5392896 | tf_op jit(solution)/shard_map/dot_general | solution.py:101
  218.2 2.0 copy.56
  (20 shorter events, 0.1 us)
Async XLA Ops:
  8.2 9.4 %copy-start.3 = (s32[32,16]{0,1:T(8,128)S(1)}, s32[32,16]{0,1:T(8,128)}, u32[]{:S(2)}) copy-start(s32[32,16]{0,1:T(8,128)} %param.12) | copy-start | bytes 6148
  8.3 9.6 %copy-start = (f32[4,16,4,2063]{3,2,1,0:T(4,128)S(1)}, f32[4,16,4,2063]{3,2,1,0:T(4,128)}, u32[]{:S(2)}) copy-start(f32[4,16,4,2063]{3,2,1,0:T(4,128)} %param.10) | copy-start | bytes 6337540
  44.6 1.6 copy-start.1
  44.6 2.2 copy-start.2
  46.8 13.8 %copy-start.4 = (s32[1,72,1]{1,2,0:T(1,128)S(1)}, s32[1,72,1]{1,2,0:T(1,128)}, u32[]{:S(2)}) copy-start(s32[1,72,1]{1,2,0:T(1,128)} %param.13) | copy-start | bytes 868
  46.8 14.0 %copy-start.6 = (s32[36]{0:T(128)S(1)}, s32[36]{0:T(128)}, u32[]{:S(2)}) copy-start(s32[36]{0:T(128)} %constant.70) | copy-start | bytes 436
  46.8 14.0 %copy-start.5 = (s32[36]{0:T(128)S(1)}, s32[36]{0:T(128)}, u32[]{:S(2)}) copy-start(s32[36]{0:T(128)} %constant.71) | copy-start | bytes 436
  50.4 15.0 %all-to-all-start = ((bf16[4,16,512]{2,0,1:T(4,128)(2,1)}), bf16[4,16,512]{2,0,1:T(4,128)(2,1)S(1)}, u32[]{:S(2)}, u32[]{:S(2)}) async-start(bf16[4,16,512]{2,0,1:T(4,128)(2,1)} %copy.46), calls=%async_computation | async-start | bytes 131072 | tf_op jit(solution)/shard_map/all_to_all | solution.py:125
  73.9 60.9 %all-to-all-start.1 = ((f32[64,2,8,512]{3,2,1,0:T(8,128)}), f32[64,2,8,512]{3,2,1,0:T(8,128)S(1)}, u32[]{:S(2)}, u32[]{:S(2)}) async-start(f32[64,2,8,512]{3,2,1,0:T(8,128)} %copy.50), calls=%async_computation.1 | async-start | bytes 4194304 | tf_op jit(solution)/shard_map/all_to_all | solution.py:132
  85.9 126.2 %all-reduce.3.cloned.1.call-start = ((), (), s32[]{:S(2)}) async-start(), calls=%async_computation.3 | async-start | bytes 4194304
  138.3 23.5 %all-to-all-start.2 = ((f32[64,2,8]{2,1,0:T(2,128)}), f32[64,2,8]{2,1,0:T(2,128)S(1)}, u32[]{:S(2)}, u32[]{:S(2)}) async-start(f32[64,2,8]{2,1,0:T(2,128)} %copy.54), calls=%async_computation.2 | async-start | bytes 131072 | tf_op jit(solution)/shard_map/all_to_all | solution.py:133
Sparse Core Ops, SparseCore 0:
  137.4 74.5 all-reduce.2
where the time goes:
time: 228 us; the launch traced here: 227 us
  waiting for transfers between devices  102 us (45%)
  other arithmetic  48.4 us (21%)
  starting transfers between devices  34.7 us (15%)
  local copies, waits for them, and re-layouts  17.1 us (8%)
  between operations  13.7 us (6%)
  matrix products  11.3 us (5%)
    unnamed x2, waiting for transfers between devices  50.1 us
    all_to_all x1, waiting for transfers between devices, local(): lax.all_to_all(partial_value, 'grp', split_axis=0, concat_axis=0, tiled=T...  46.9 us
    reduce_sum x2, other arithmetic, decimate(): jnp.sum(segment_part * fir_taps[None, None, :, offset:offset + 1], axis=2)  26.7 us
    all_to_all x1, starting transfers between devices, local(): lax.all_to_all(count_buffer, 'grp', split_axis=0, concat_axis=0, tiled=True)  12.3 us
    all_to_all x1, starting transfers between devices, local(): lax.all_to_all(partial_value, 'grp', split_axis=0, concat_axis=0, tiled=T...  12 us
    all_to_all x1, starting transfers between devices, local(): lax.all_to_all(spectra, 'sta', split_axis=1, concat_axis=0, tiled=True)  10.1 us
    cos x1, other arithmetic, lag_table(): return jnp.concatenate([jnp.cos(radians), -jnp.sin(radians)], axis=0)  9.53 us
    cos x1, other arithmetic, forward_table(): return jnp.concatenate([jnp.cos(radians), -jnp.sin(radians)], axis=1)  9.38 us
  transfers between devices with their start and end apart: 4, of which 4 were waited for; matrix products, arithmetic and copies ran while one was open for 6% of the time, Pallas kernels for 0%

commit v1 on v0

v1 whole, which is shorter than its diff:
```python
import math

import jax
import jax.numpy as jnp
import numpy as np
from jax import lax
from jax.sharding import PartitionSpec as P

SEG = 2048
NB = 256
K0 = 16
SMOOTH = 32
MAXLAG = 1000
CAP = 2
SPLIT = 2
STEP = 64

EPSILON = 1e-06
PRECISE = lax.Precision.HIGHEST
FREQS = K0 + np.arange(NB)


def turn(multiples):
    angle = (np.asarray(multiples)[:, None] * FREQS[None, :] % (2 * SEG)) * (math.pi / SEG)
    return np.cos(angle).astype(np.float32), (-np.sin(angle)).astype(np.float32)


def wave_table():
    coarse_re, coarse_im = turn(STEP * np.arange(SEG // STEP))
    fine_re, fine_im = turn(np.arange(STEP))
    cr, ci = coarse_re[:, None], coarse_im[:, None]
    fr, fi = fine_re[None], fine_im[None]
    real = jnp.asarray(cr) * fr - jnp.asarray(ci) * fi
    imag = jnp.asarray(cr) * fi + jnp.asarray(ci) * fr
    return jnp.concatenate([real.reshape(SEG, NB), imag.reshape(SEG, NB)], axis=1)


def smoother():
    near = np.abs(np.arange(NB)[:, None] - np.arange(NB)[None, :]) <= SMOOTH
    return near.astype(np.float32) / (2 * SMOOTH + 1)


def spectra_of(seismograms, fir_taps, table):
    stations, windows, phases, _ = seismograms.shape
    taps = fir_taps.shape[1]
    rows = stations * windows
    raw = seismograms.reshape(rows, phases, -1)
    main = raw[:, :, :SEG].reshape(rows * phases, SEG)
    whole = jnp.dot(main, table, precision=lax.Precision.HIGH, preferred_element_type=jnp.float32)
    whole = whole.reshape(rows, phases, 2 * NB)
    whole_re, whole_im = whole[..., :NB], whole[..., NB:]
    adv_re, adv_im = turn(-np.arange(taps))
    gain_re = jnp.dot(fir_taps, adv_re, precision=PRECISE)
    gain_im = jnp.dot(fir_taps, adv_im, precision=PRECISE)
    real = jnp.sum(whole_re * gain_re - whole_im * gain_im, axis=1)
    imag = jnp.sum(whole_re * gain_im + whole_im * gain_re, axis=1)
    padded = jnp.pad(fir_taps, ((0, 0), (0, taps)))
    shifted = jnp.stack([padded[:, j : j + taps - 1] for j in range(1, taps)], axis=-1)
    shifted = shifted.reshape(phases * (taps - 1), taps - 1)
    head = jnp.dot(raw[:, :, : taps - 1].reshape(rows, -1), shifted, precision=PRECISE)
    tail = jnp.dot(raw[:, :, SEG:].reshape(rows, -1), shifted, precision=PRECISE)
    sign = np.where(FREQS % 2 == 0, 1.0, -1.0).astype(np.float32)
    edge = np.concatenate([adv_re[1:], adv_im[1:]], axis=1)
    edges = np.concatenate([-edge, edge * np.concatenate([sign, sign])], axis=0)
    fix = jnp.dot(jnp.concatenate([head, tail], axis=1), edges, precision=PRECISE)
    return real + fix[:, :NB], imag + fix[:, NB:]


def local(seismograms, fir_taps, valid_windows, pair_owners):
    stations, windows = seismograms.shape[:2]
    members = lax.axis_size("sta")
    groups = lax.axis_size("grp")
    member = lax.axis_index("sta")
    table = wave_table()
    real, imag = spectra_of(seismograms, fir_taps, table)
    own_valid = lax.dynamic_slice_in_dim(valid_windows, member * stations, stations, 0)
    smoothed = jnp.dot(real * real + imag * imag, smoother(), precision=PRECISE)
    whitener = own_valid.reshape(-1, 1).astype(jnp.float32) / jnp.sqrt(smoothed + EPSILON)
    white = jnp.concatenate([real * whitener, imag * whitener], axis=1).astype(jnp.bfloat16)
    white = white.reshape(stations, windows, 2 * NB)
    gathered = lax.all_gather(white, "sta", axis=0, tiled=False)

    side_a, side_c = member // stations, member % stations
    left_rows = stations // SPLIT
    left = gathered.reshape(members, SPLIT, left_rows, windows, 2 * NB)
    left = lax.dynamic_index_in_dim(left, side_a, 2, keepdims=False).astype(jnp.float32)
    right = lax.dynamic_index_in_dim(gathered, side_c, 1, keepdims=False).astype(jnp.float32)
    lr, li = left[:, :, None, :, :NB], left[:, :, None, :, NB:]
    rr, ri = right[None, None, :, :, :NB], right[None, None, :, :, NB:]
    stack_re = jnp.sum(lr * rr + li * ri, axis=3)
    stack_im = jnp.sum(li * rr - lr * ri, axis=3)
    mask = valid_windows.astype(jnp.float32)
    mask_left = mask.reshape(members, SPLIT, left_rows, windows)
    mask_left = lax.dynamic_index_in_dim(mask_left, side_a, 2, keepdims=False)
    mask_right = mask.reshape(members, stations, windows)
    mask_right = lax.dynamic_index_in_dim(mask_right, side_c, 1, keepdims=False)
    count = jnp.einsum("ihw,jw->ihj", mask_left, mask_right, precision=PRECISE)
    scale = (1.0 / (math.sqrt(NB) * jnp.maximum(count, 1.0)))[..., None]
    lead_re, lead_im = turn([MAXLAG])
    moved_re = (stack_re * lead_re - stack_im * lead_im) * scale
    moved_im = (stack_re * lead_im + stack_im * lead_re) * scale
    combos = members * SPLIT * members
    moved = jnp.concatenate([moved_re, moved_im], axis=-1).reshape(combos, 2 * NB)
    moved = moved.astype(jnp.bfloat16)

    rows_of, cols_of = np.triu_indices(members)
    pair_i = np.repeat(rows_of, SPLIT)
    pair_j = np.repeat(cols_of, SPLIT)
    pair_h = np.tile(np.arange(SPLIT), rows_of.shape[0])
    combo_of = (pair_i * SPLIT + pair_h) * members + pair_j
    owners = pair_owners[0, :, 0]
    blocks = owners.shape[0]
    earlier = np.arange(blocks)[None, :] < np.arange(blocks)[:, None]
    slot = jnp.sum((earlier & (owners[:, None] == owners[None, :])).astype(jnp.int32), axis=1)
    place = owners * CAP + slot
    spread = np.zeros((blocks, combos), np.float32)
    spread[np.arange(blocks), combo_of] = 1.0
    onto = (place[None, :] == jnp.arange(groups * CAP, dtype=jnp.int32)[:, None])
    onto = jnp.dot(onto.astype(jnp.bfloat16), jnp.asarray(spread, jnp.bfloat16), preferred_element_type=jnp.float32)
    routed = jnp.dot(onto.astype(jnp.bfloat16), moved, preferred_element_type=jnp.float32)
    routed = routed.astype(jnp.bfloat16).reshape(groups, CAP, 2 * NB)
    arrived = lax.all_to_all(routed, "grp", split_axis=0, concat_axis=0, tiled=True)
    waves = table.astype(jnp.bfloat16)[: 2 * MAXLAG + 1]
    lagged = lax.dot_general(
        arrived.reshape(groups * CAP, 2 * NB),
        waves,
        (((1,), (1,)), ((), ())),
        preferred_element_type=jnp.float32,
    )
    return lagged.reshape(1, groups, CAP, 1, 2 * MAXLAG + 1)


def solution(mesh):
    in_specs = (P(("grp", "sta"), None, None, None), P(), P("grp", None), P("grp", None, None))
    out_specs = P("grp", None, None, "sta", None)
    return jax.shard_map(local, mesh=mesh, in_specs=in_specs, out_specs=out_specs, check_vma=False)
```

time: 228 us -> 66.8 us (0.29)
  waiting for transfers between devices: 102 us -> 0 us
  other arithmetic: 48.4 us -> 2.53 us
  blocking collectives: 0 us -> 42.4 us
  starting transfers between devices: 34.7 us -> 0 us
  between operations: 13.7 us -> 0.39 us
  matrix products: 11.3 us -> 6.39 us
  local copies, waits for them, and re-layouts: 17.1 us -> 14.5 us
    all_to_all x3 -> x0, waiting for transfers between devices: 51.9 us -> none  [the longest x1 46.9 us: local(): lax.all_to_all(partial_value, 'grp', split_axis=0, concat_axis=0, tiled=T...]
    unnamed x2 -> x0, waiting for transfers between devices: 50.1 us -> none
    all_to_all x3 -> x0, starting transfers between devices: 34.4 us -> none  [the longest x1 12.3 us: local(): lax.all_to_all(count_buffer, 'grp', split_axis=0, concat_axis=0, tiled=True)]
    reduce_sum x4 -> x3, other arithmetic: 28.2 us -> 1.88 us  [the longest x1 1.31 us: local(): stack_re = jnp.sum(lr * rr + li * ri, axis=3)]
    all_to_all x0 -> x1, blocking collectives: none -> 22.6 us  [local(): lax.all_to_all(routed, 'grp', split_axis=0, concat_axis=0, tiled=True)]
    all_gather x0 -> x1, blocking collectives: none -> 19.8 us  [local(): gathered = lax.all_gather(white, 'sta', axis=0, tiled=False)]
    cos x2 -> x0, other arithmetic: 18.9 us -> none  [the longest x1 9.53 us: lag_table(): return jnp.concatenate([jnp.cos(radians), -jnp.sin(radians)], axis=0)]
    slice x1 -> x6, local copies, waits for them, and re-layouts: 1.71 us -> 6.69 us  [the longest x2 4.55 us: spectra_of(): main = raw[:, :, :SEG].reshape(rows * phases, SEG)]
  transfers between devices with their start and end apart: 4 -> 0, of which waited for: 4 -> 0; matrix products, arithmetic and copies ran while one was open for 6% -> 0% of each run, Pallas kernels for 0% -> 0%
where the time goes in v1:
time: 66.8 us; the launch traced here: 66.2 us
  blocking collectives  42.4 us (63%)
  local copies, waits for them, and re-layouts  14.5 us (22%)
  matrix products  6.39 us (10%)
  other arithmetic  2.53 us (4%)
    all_to_all x1, blocking collectives, local(): lax.all_to_all(routed, 'grp', split_axis=0, concat_axis=0, tiled=True)  22.6 us
    all_gather x1, blocking collectives, local(): gathered = lax.all_gather(white, 'sta', axis=0, tiled=False)  19.8 us
    slice x2, local copies, waits for them, and re-layouts, spectra_of(): main = raw[:, :, :SEG].reshape(rows * phases, SEG)  4.55 us
    unnamed x38, local copies, waits for them, and re-layouts  3.48 us
    dot_general x1, matrix products, local(): lax.dot_general(arrived.reshape(groups * CAP, 2 * NB), waves, (((1,), (1,...  2.37 us
    slice x2, local copies, waits for them, and re-layouts, spectra_of(): padded[:, j:j + taps - 1]  2.06 us
    dot_general x1, local copies, waits for them, and re-layouts, local(): lax.dot_general(arrived.reshape(groups * CAP, 2 * NB), waves, (((1,), (1,...  2.05 us
    dot_general x1, matrix products, spectra_of(): jnp.dot(main, table, precision=lax.Precision.HIGH, preferred_element_type...  2.04 us

profile of v1, /device:TPU:1, one launch (start us, length us, event | category | flops | bytes accessed | tf_op | source)
XLA Modules:
  0.0 66.2 jit_solution(8019028965508973316)
XLA Ops:
  0.0 0.9 %pad_slice_fusion.3 = (f32[4,15]{1,0:T(4,128)S(1)}, f32[4,15]{1,0:T(4,128)S(1)}, f32[4,15]{1,0:T(4,128)S(1)}, f32[4,15]{1,0:T(4,128)S(1)}, f32[4,15]{1,0:T(4,128)S(1)}) fusion(f32[4,16]{1,0:T(4,128)} %param.17), kind=kLoop, calls=%fused_computation.67 | loop fusion | bytes 1456 | tf_op jit(solution)/shard_map/slice | solution.py:58
  0.9 1.1 %pad_slice_fusion.2 = (f32[4,15]{1,0:T(4,128)S(1)}, f32[4,15]{1,0:T(4,128)S(1)}, f32[4,15]{1,0:T(4,128)S(1)}, f32[4,15]{1,0:T(4,128)S(1)}, f32[4,15]{1,0:T(4,128...) fusion(f32[4,16]{1,0:T(4,128)} %param.17), kind=kLoop, calls=%fused_computation.66 | loop fusion | bytes 6496 | tf_op jit(solution)/shard_map/slice | solution.py:58
  2.1 1.8 %copy.100 = f32[4,16,4,2063]{3,1,0,2:T(8,128)S(1)} copy(f32[4,16,4,2063]{3,2,1,0:T(4,128)} %param.16) | data formatting | bytes 4225024 | tf_op args[0]
  3.9 0.1 stack.63
  3.9 0.2 convolution_bitcast_fusion.2
  4.1 0.2 convolution_bitcast_fusion.1
  4.4 0.0 copy-start.13
  4.4 0.0 copy-start.15
  4.4 0.0 copy-start.5
  4.4 0.0 copy-start.12
  4.4 0.0 copy-start.11
  4.4 0.0 copy-start.14
  4.5 1.6 %slice.111 = f32[64,4,2048]{2,0,1:T(8,128)} slice(f32[64,4,2063]{2,0,1:T(8,128)S(1)} %bitcast.119), slice={[0:64], [0:4], [0:2048]} | slice | bytes 4194304 | tf_op jit(solution)/shard_map/slice | solution.py:48
  6.1 0.2 convert_reduce_fusion
  6.3 0.1 convolution_bitcast_fusion.4
  6.4 0.1 convolution_bitcast_fusion.3
  6.5 0.1 copy.119
  6.6 0.1 convert_element_type.53
  6.8 0.1 fusion.9
  6.9 0.1 mul.258
  7.0 2.9 %copy.101 = f32[64,4,2048]{2,1,0:T(4,128)S(1)} copy(f32[64,4,2048]{2,0,1:T(8,128)} %slice.111) | data formatting | bytes 4194304 | tf_op jit(solution)/shard_map/slice | solution.py:48
  10.0 0.0 copy-start.3
  10.0 0.0 copy-start.4
  10.0 0.0 copy-start.6
  10.0 0.0 copy-start.7
  10.0 1.8 %reshape.124 = f32[256,2048]{1,0:T(8,128)} reshape(f32[64,4,2048]{2,1,0:T(4,128)S(1)} %copy.101) | data formatting | bytes 4194304 | tf_op jit(solution)/shard_map/reshape | solution.py:48
  11.8 0.5 multiply_subtract_fusion
  12.3 1.3 %copy-done = f32[32,64,256]{2,1,0:T(8,128)} copy-done((f32[32,64,256]{2,1,0:T(8,128)}, f32[32,64,256]{2,1,0:T(8,128)S(1)}, u32[]{:S(2)}) %copy-start) | copy-done | bytes 2097176
  13.6 0.1 copy-done.1
  13.7 2.0 %fusion.5 = f32[256,512]{1,0:T(8,128)S(1)} fusion(f32[256,2048]{1,0:T(8,128)S(1)} %copy-done.1, f32[2048,256]{1,0:T(8,128)S(1)} %bitcast.122, f32[2048,256]{1,0:T(8,128)S(1)} %bitcast.120), kind=kOutput, calls=%fused_computation.12 | convolution fusion | flops 1611661312 | bytes 6815744 | tf_op jit(solution)/shard_map/dot_general | solution.py:49
  15.8 0.0 copy-start.2
  15.8 0.1 reshape.125
  16.0 0.3 fusion.34
  16.3 0.3 convolution_add_fusion
  16.6 0.4 add_reduce_fusion.1
  17.0 0.3 multiply_convert_fusion.1
  17.3 0.0 copy-start.16
  17.3 0.0 copy-start.17
  17.3 19.8 %all_gather.3 = bf16[8,4,16,512]{3,2,1,0:T(8,128)(2,1)S(1)} all-gather(bf16[1,4,16,512]{3,2,1,0:T(8,128)(2,1)S(1)} %pad_maximum_fusion.4), channel_id=1, replica_groups=mesh['grp'=64,'sta'=8] {'sta'}, dimensions={0}, use_global_device_ids=true | all-gather | bytes 589824 | tf_op jit(solution)/shard_map/all_gather | solution.py:81
  37.2 0.1 bitcast_convert_fusion
  37.3 0.1 fusion.32
  37.4 1.3 %add_reduce_fusion = (f32[8,2,8,256]{3,2,1,0:T(8,128)S(1)}, f32[8,2,8,256]{3,2,1,0:T(8,128)S(1)}) fusion(f32[8,16,256]{2,1,0:T(8,128)S(1)} %get-tuple-element.14, f32[8,2,16,256]{3,2,1,0:T(8,128)S(1)} %get-tuple-element.10, f32[8,16,256]{2,1,0:T(8,128)S(1)} %get-tuple-element.13, f32[8,2,16,256]{3,2,1,0:T(8,128)S(1)} %get-tuple-element.9), kind=kLoop, calls=%fused_computation.8 | loop fusion | flops 4128768 | bytes 1048576 | tf_op jit(solution)/shard_map/reduce_sum | solution.py:90
  38.7 0.1 fusion.17
  38.8 0.3 convolution_convert_fusion
  39.1 0.1 reshape.129
  39.2 22.6 %all_to_all.5 = bf16[64,2,512]{2,1,0:T(2,128)(2,1)S(1)} all-to-all(bf16[64,2,512]{2,1,0:T(2,128)(2,1)S(1)} %reshape.129), channel_id=1, replica_groups=mesh['grp'=64,'sta'=8] {'grp'}, dimensions={0} | all-to-all | bytes 262144 | tf_op jit(solution)/shard_map/all_to_all | solution.py:122
  61.7 2.4 %convolution_bitcast_fusion = f32[1,64,2,1,2001]{4,1,2,3,0:T(8,128)S(1)} fusion(f32[2048,256]{1,0:T(8,128)} %bitcast.123, f32[2048,256]{1,0:T(8,128)S(1)} %bitcast.121, bf16[64,2,512]{2,1,0:T(2,128)(2,1)S(1)} %all_to_all.5), kind=kOutput, calls=%fused_computation.6 | convolution fusion | flops 266373120 | bytes 5349888 | tf_op jit(solution)/shard_map/dot_general | solution.py:124
  64.1 2.1 %copy.124 = f32[1,64,2,1,2001]{4,3,2,1,0:T(1,128)} copy(f32[1,64,2,1,2001]{4,1,2,3,0:T(8,128)S(1)} %convolution_bitcast_fusion) | data formatting | bytes 2049024 | tf_op jit(solution)/shard_map/dot_general | solution.py:124
  (30 shorter events, 0.1 us)
Async XLA Ops:
  4.4 1.7 %copy-start.13 = (pred[72,72]{1,0:T(8,128)(4,1)S(1)}, pred[72,72]{1,0:T(8,128)(4,1)}, u32[]{:S(2)}) copy-start(pred[72,72]{1,0:T(8,128)(4,1)} %constant.93.clone) | copy-start | bytes 15556
  4.4 1.7 %copy-start.15 = (s32[1,72,1]{1,2,0:T(1,128)S(1)}, s32[1,72,1]{1,2,0:T(1,128)}, u32[]{:S(2)}) copy-start(s32[1,72,1]{1,2,0:T(1,128)} %param.19) | copy-start | bytes 868
  4.4 1.8 %copy-start.5 = (f32[4,16]{1,0:T(4,128)S(1)}, f32[4,16]{1,0:T(4,128)}, u32[]{:S(2)}) copy-start(f32[4,16]{1,0:T(4,128)} %param.17) | copy-start | bytes 772
  4.4 1.8 %copy-start.12 = (f32[16,256]{1,0:T(8,128)S(1)}, f32[16,256]{1,0:T(8,128)}, u32[]{:S(2)}) copy-start(f32[16,256]{1,0:T(8,128)} %constant.87.clone) | copy-start | bytes 49156
  4.4 2.0 %copy-start.11 = (f32[16,256]{1,0:T(8,128)S(1)}, f32[16,256]{1,0:T(8,128)}, u32[]{:S(2)}) copy-start(f32[16,256]{1,0:T(8,128)} %constant.88.clone) | copy-start | bytes 49156
  4.4 2.1 %copy-start.14 = (s32[32,16]{0,1:T(8,128)S(1)}, s32[32,16]{0,1:T(8,128)}, u32[]{:S(2)}) copy-start(s32[32,16]{0,1:T(8,128)} %param.18) | copy-start | bytes 6148
  10.0 1.8 %copy-start.3 = (f32[64,256]{1,0:T(8,128)S(1)}, f32[64,256]{1,0:T(8,128)}, u32[]{:S(2)}) copy-start(f32[64,256]{1,0:T(8,128)} %constant.103) | copy-start | bytes 196612
  10.0 1.8 %copy-start.4 = (f32[64,256]{1,0:T(8,128)S(1)}, f32[64,256]{1,0:T(8,128)}, u32[]{:S(2)}) copy-start(f32[64,256]{1,0:T(8,128)} %constant.101) | copy-start | bytes 196612
  10.0 1.8 %copy-start.6 = (f32[32,256]{1,0:T(8,128)S(1)}, f32[32,256]{1,0:T(8,128)}, u32[]{:S(2)}) copy-start(f32[32,256]{1,0:T(8,128)} %constant.102) | copy-start | bytes 98308
  10.0 1.8 %copy-start.7 = (f32[32,256]{1,0:T(8,128)S(1)}, f32[32,256]{1,0:T(8,128)}, u32[]{:S(2)}) copy-start(f32[32,256]{1,0:T(8,128)} %constant.100) | copy-start | bytes 98308
  11.8 1.9 %copy-start.1 = (f32[256,2048]{1,0:T(8,128)S(1)}, f32[256,2048]{1,0:T(8,128)}, u32[]{:S(2)}) copy-start(f32[256,2048]{1,0:T(8,128)} %reshape.124) | copy-start | bytes 6291460
  12.2 1.3 %copy-start = (f32[32,64,256]{2,1,0:T(8,128)}, f32[32,64,256]{2,1,0:T(8,128)S(1)}, u32[]{:S(2)}) copy-start(f32[32,64,256]{2,1,0:T(8,128)S(1)} %get-tuple-element.18) | copy-start | bytes 6291460
  13.7 2.2 %copy-start.9 = (f32[15,512]{1,0:T(8,128)S(1)}, f32[15,512]{1,0:T(8,128)}, u32[]{:S(2)}) copy-start(f32[15,512]{1,0:T(8,128)} %constant.104) | copy-start | bytes 92164
  13.7 2.6 %copy-start.8 = (f32[15,512]{1,0:T(8,128)S(1)}, f32[15,512]{1,0:T(8,128)}, u32[]{:S(2)}) copy-start(f32[15,512]{1,0:T(8,128)} %constant.105) | copy-start | bytes 92164
  15.8 1.2 %copy-start.2 = (f32[256,256]{1,0:T(8,128)S(1)}, f32[256,256]{1,0:T(8,128)}, u32[]{:S(2)}) copy-start(f32[256,256]{1,0:T(8,128)} %constant.90.clone) | copy-start | bytes 786436
  17.3 21.4 %copy-start.16 = (f32[256]{0:T(256)S(1)}, f32[256]{0:T(256)}, u32[]{:S(2)}) copy-start(f32[256]{0:T(256)} %constant.107) | copy-start | bytes 3076
  17.3 21.4 %copy-start.17 = (f32[256]{0:T(256)S(1)}, f32[256]{0:T(256)}, u32[]{:S(2)}) copy-start(f32[256]{0:T(256)} %constant.106) | copy-start | bytes 3076
  37.2 1.6 %copy-start.10 = (bf16[72,128]{1,0:T(8,128)(2,1)S(1)}, bf16[72,128]{1,0:T(8,128)(2,1)}, u32[]{:S(2)}) copy-start(bf16[72,128]{1,0:T(8,128)(2,1)} %constant.94.clone) | copy-start | bytes 55300

commit v2 on v1

--- a/solution.py
+++ b/solution.py
@@ -1,9 +1,12 @@
+import functools
 import math
 
 import jax
 import jax.numpy as jnp
 import numpy as np
 from jax import lax
+from jax.experimental import pallas as pl
+from jax.experimental.pallas import tpu as pltpu
 from jax.sharding import PartitionSpec as P
 
 SEG = 2048
@@ -66,6 +69,122 @@
     return real + fix[:, :NB], imag + fix[:, NB:]
 
 
+def combine(members, groups, stations, windows, *refs):
+    (spec_ref, valid_ref, smooth_ref, lead_ref, scale_ref, onto_ref, out_ref) = refs[:7]
+    white, left, right, stack, staged, routed, arrived = refs[7:14]
+    near_send, near_recv, far_send, far_recv = refs[14:]
+    mine = lax.axis_index("sta")
+    group = lax.axis_index("grp")
+    half = stations // SPLIT
+
+    barrier = pltpu.get_barrier_semaphore()
+
+    @pl.loop(1, groups)
+    def _(k):
+        pl.semaphore_signal(
+            barrier,
+            inc=1,
+            device_id={"grp": lax.rem(group + k, groups)},
+            device_id_type=pl.DeviceIdType.MESH,
+        )
+
+    @pl.loop(1, members)
+    def _(k):
+        pl.semaphore_signal(
+            barrier,
+            inc=1,
+            device_id={"sta": lax.rem(mine + k, members)},
+            device_id_type=pl.DeviceIdType.MESH,
+        )
+
+    real, imag = spec_ref[:, :NB], spec_ref[:, NB:]
+    smoothed = jnp.dot(
+        real * real + imag * imag,
+        smooth_ref[...],
+        precision=PRECISE,
+        preferred_element_type=jnp.float32,
+    )
+    whitener = valid_ref[...] / jnp.sqrt(smoothed + EPSILON)
+    white[:, :, :NB] = (real * whitener).astype(jnp.bfloat16).reshape(stations, windows, NB)
+    white[:, :, NB:] = (imag * whitener).astype(jnp.bfloat16).reshape(stations, windows, NB)
+
+    def near(k):
+        peer = lax.rem(mine + k, members)
+        side_a, side_c = peer // stations, lax.rem(peer, stations)
+        copies = []
+        for part in range(SPLIT + 1):
+            station = side_c if part == SPLIT else part * half + side_a
+            into = right.at[mine] if part == SPLIT else left.at[mine, part]
+            copies.append(
+                pltpu.make_async_remote_copy(
+                    src_ref=white.at[station],
+                    dst_ref=into,
+                    send_sem=near_send.at[k, part],
+                    recv_sem=near_recv.at[k, part],
+                    device_id={"sta": peer},
+                    device_id_type=pl.DeviceIdType.MESH,
+                )
+            )
+        return copies
+
+    pl.semaphore_wait(barrier, members - 1 + groups - 1)
+    for k in range(1, members):
+        for copy in near(k):
+            copy.start()
+    for part in range(SPLIT):
+        left[mine, part] = white[part * half + mine // stations]
+    right[mine] = white[lax.rem(mine, stations)]
+    for k in range(1, members):
+        for copy in near(k):
+            copy.wait()
+
+    @pl.loop(0, members * SPLIT)
+    def _(n):
+        i, h = n // SPLIT, lax.rem(n, SPLIT)
+        ours = left[i, h].astype(jnp.float32)
+        theirs = right[...].astype(jnp.float32)
+        lr, li = ours[None, :, :NB], ours[None, :, NB:]
+        rr, ri = theirs[:, :, :NB], theirs[:, :, NB:]
+        rows = pl.ds(pl.multiple_of(n * members, members), members)
+        stack[rows, :NB] = jnp.sum(lr * rr + li * ri, axis=1)
+        stack[rows, NB:] = jnp.sum(li * rr - lr * ri, axis=1)
+
+    lead_re, lead_im = lead_ref[0:1], lead_ref[1:2]
+    stack_re, stack_im = stack[:, :NB], stack[:, NB:]
+    moved_re = ((stack_re * lead_re - stack_im * lead_im) * scale_ref[...]).astype(jnp.bfloat16)
+    moved_im = ((stack_re * lead_im + stack_im * lead_re) * scale_ref[...]).astype(jnp.bfloat16)
+    for slot in range(CAP):
+        for part, moved in enumerate((moved_re, moved_im)):
+            placed = jnp.dot(onto_ref[slot], moved, preferred_element_type=jnp.float32)
+            for chunk in range(NB // 128):
+                row = slot * (2 * NB // 128) + part * (NB // 128) + chunk
+                staged[:, row, :] = placed[:, chunk * 128 : (chunk + 1) * 128]
+    routed[...] = staged[...].astype(jnp.bfloat16)
+
+    def far(k):
+        peer = lax.rem(group + k, groups)
+        return pltpu.make_async_remote_copy(
+            src_ref=routed.at[peer],
+            dst_ref=arrived.at[group],
+            send_sem=far_send.at[k],
+            recv_sem=far_recv.at[k],
+            device_id={"grp": peer},
+            device_id_type=pl.DeviceIdType.MESH,
+        )
+
+    @pl.loop(1, groups)
+    def _(k):
+        far(k).start()
+
+    arrived[group] = routed[group]
+
+    @pl.loop(1, groups)
+    def _(k):
+        far(k).wait()
+
+    out_ref[...] = arrived[...]
+
+
 def local(seismograms, fir_taps, valid_windows, pair_owners):
     stations, windows = seismograms.shape[:2]
     members = lax.axis_size("sta")
@@ -74,34 +193,19 @@
     table = wave_table()
     real, imag = spectra_of(seismograms, fir_taps, table)
     own_valid = lax.dynamic_slice_in_dim(valid_windows, member * stations, stations, 0)
-    smoothed = jnp.dot(real * real + imag * imag, smoother(), precision=PRECISE)
-    whitener = own_valid.reshape(-1, 1).astype(jnp.float32) / jnp.sqrt(smoothed + EPSILON)
-    white = jnp.concatenate([real * whitener, imag * whitener], axis=1).astype(jnp.bfloat16)
-    white = white.reshape(stations, windows, 2 * NB)
-    gathered = lax.all_gather(white, "sta", axis=0, tiled=False)
+    own_valid = own_valid.reshape(-1, 1).astype(jnp.float32)
 
     side_a, side_c = member // stations, member % stations
     left_rows = stations // SPLIT
-    left = gathered.reshape(members, SPLIT, left_rows, windows, 2 * NB)
-    left = lax.dynamic_index_in_dim(left, side_a, 2, keepdims=False).astype(jnp.float32)
-    right = lax.dynamic_index_in_dim(gathered, side_c, 1, keepdims=False).astype(jnp.float32)
-    lr, li = left[:, :, None, :, :NB], left[:, :, None, :, NB:]
-    rr, ri = right[None, None, :, :, :NB], right[None, None, :, :, NB:]
-    stack_re = jnp.sum(lr * rr + li * ri, axis=3)
-    stack_im = jnp.sum(li * rr - lr * ri, axis=3)
     mask = valid_windows.astype(jnp.float32)
     mask_left = mask.reshape(members, SPLIT, left_rows, windows)
     mask_left = lax.dynamic_index_in_dim(mask_left, side_a, 2, keepdims=False)
     mask_right = mask.reshape(members, stations, windows)
     mask_right = lax.dynamic_index_in_dim(mask_right, side_c, 1, keepdims=False)
+    combos = members * SPLIT * members
     count = jnp.einsum("ihw,jw->ihj", mask_left, mask_right, precision=PRECISE)
-    scale = (1.0 / (math.sqrt(NB) * jnp.maximum(count, 1.0)))[..., None]
-    lead_re, lead_im = turn([MAXLAG])
-    moved_re = (stack_re * lead_re - stack_im * lead_im) * scale
-    moved_im = (stack_re * lead_im + stack_im * lead_re) * scale
-    combos = members * SPLIT * members
-    moved = jnp.concatenate([moved_re, moved_im], axis=-1).reshape(combos, 2 * NB)
-    moved = moved.astype(jnp.bfloat16)
+    scale = (1.0 / (math.sqrt(NB) * jnp.maximum(count, 1.0))).reshape(combos, 1)
+    lead = jnp.asarray(np.concatenate(turn([MAXLAG])))
 
     rows_of, cols_of = np.triu_indices(members)
     pair_i = np.repeat(rows_of, SPLIT)
@@ -112,14 +216,36 @@
     blocks = owners.shape[0]
     earlier = np.arange(blocks)[None, :] < np.arange(blocks)[:, None]
     slot = jnp.sum((earlier & (owners[:, None] == owners[None, :])).astype(jnp.int32), axis=1)
-    place = owners * CAP + slot
+    place = slot * groups + owners
     spread = np.zeros((blocks, combos), np.float32)
     spread[np.arange(blocks), combo_of] = 1.0
     onto = (place[None, :] == jnp.arange(groups * CAP, dtype=jnp.int32)[:, None])
     onto = jnp.dot(onto.astype(jnp.bfloat16), jnp.asarray(spread, jnp.bfloat16), preferred_element_type=jnp.float32)
-    routed = jnp.dot(onto.astype(jnp.bfloat16), moved, preferred_element_type=jnp.float32)
-    routed = routed.astype(jnp.bfloat16).reshape(groups, CAP, 2 * NB)
-    arrived = lax.all_to_all(routed, "grp", split_axis=0, concat_axis=0, tiled=True)
+    onto = onto.astype(jnp.bfloat16).reshape(CAP, groups, combos)
+
+    vmem = pl.BlockSpec(memory_space=pltpu.VMEM)
+    tile = (groups, CAP * 2 * NB // 128, 128)
+    arrived = pl.pallas_call(
+        functools.partial(combine, members, groups, stations, windows),
+        out_shape=jax.ShapeDtypeStruct(tile, jnp.bfloat16),
+        in_specs=[vmem] * 6,
+        out_specs=vmem,
+        scratch_shapes=[
+            pltpu.VMEM((stations, windows, 2 * NB), jnp.bfloat16),
+            pltpu.VMEM((members, SPLIT, windows, 2 * NB), jnp.bfloat16),
+            pltpu.VMEM((members, windows, 2 * NB), jnp.bfloat16),
+            pltpu.VMEM((combos, 2 * NB), jnp.float32),
+            pltpu.VMEM(tile, jnp.float32),
+            pltpu.VMEM(tile, jnp.bfloat16),
+            pltpu.VMEM(tile, jnp.bfloat16),
+            pltpu.SemaphoreType.DMA((members, SPLIT + 1)),
+            pltpu.SemaphoreType.DMA((members, SPLIT + 1)),
+            pltpu.SemaphoreType.DMA((groups,)),
+            pltpu.SemaphoreType.DMA((groups,)),
+        ],
+        compiler_params=pltpu.CompilerParams(collective_id=0, has_side_effects=True),
+        name="combine",
+    )(jnp.concatenate([real, imag], axis=1), own_valid, jnp.asarray(smoother()), lead, scale, onto)
     waves = table.astype(jnp.bfloat16)[: 2 * MAXLAG + 1]
     lagged = lax.dot_general(
         arrived.reshape(groups * CAP, 2 * NB),

time: 66.8 us -> 60.6 us (0.907)
  blocking collectives: 42.4 us -> 0 us
  Pallas kernels: 0 us -> 35.5 us
  local copies, waits for them, and re-layouts: 14.5 us -> 16.1 us
  other arithmetic: 2.53 us -> 1.74 us
    pallas_call x0 -> x1, Pallas kernels: none -> 35.5 us  [local(): pl.pallas_call(functools.partial(combine, members, groups, stations, wind...]
    all_to_all x1 -> x0, blocking collectives: 22.6 us -> none  [local(): lax.all_to_all(routed, 'grp', split_axis=0, concat_axis=0, tiled=True)]
    all_gather x1 -> x0, blocking collectives: 19.8 us -> none  [local(): gathered = lax.all_gather(white, 'sta', axis=0, tiled=False)]
    slice x2, local copies, waits for them, and re-layouts: 4.55 us -> 2.94 us  [spectra_of(): main = raw[:, :, :SEG].reshape(rows * phases, SEG)]
    reduce_sum x2 -> x1, other arithmetic: 1.71 us -> 0.42 us  [spectra_of(): real = jnp.sum(whole_re * gain_re - whole_im * gain_im, axis=1)]
    reshape x1, local copies, waits for them, and re-layouts: 1.75 us -> 3 us  [spectra_of(): main = raw[:, :, :SEG].reshape(rows * phases, SEG)]
    another operation x0 -> x1, local copies, waits for them, and re-layouts: none -> 0.96 us
    unnamed x38 -> x32, local copies, waits for them, and re-layouts: 3.48 us -> 3.44 us
where the time goes in v2:
time: 60.6 us; the launch traced here: 60.2 us
  Pallas kernels  35.5 us (59%)
  local copies, waits for them, and re-layouts  16.1 us (27%)
  matrix products  6.6 us (11%)
  other arithmetic  1.74 us (3%)
    pallas_call x1, Pallas kernels, local(): pl.pallas_call(functools.partial(combine, members, groups, stations, wind...  35.5 us
    unnamed x32, local copies, waits for them, and re-layouts  3.44 us
    reshape x1, local copies, waits for them, and re-layouts, spectra_of(): main = raw[:, :, :SEG].reshape(rows * phases, SEG)  3 us
    slice x2, local copies, waits for them, and re-layouts, spectra_of(): main = raw[:, :, :SEG].reshape(rows * phases, SEG)  2.94 us
    dot_general x1, matrix products, local(): lax.dot_general(arrived.reshape(groups * CAP, 2 * NB), waves, (((1,), (1,...  2.38 us
    slice x2, local copies, waits for them, and re-layouts, spectra_of(): padded[:, j:j + taps - 1]  2.06 us
    dot_general x1, local copies, waits for them, and re-layouts, local(): lax.dot_general(arrived.reshape(groups * CAP, 2 * NB), waves, (((1,), (1,...  2.05 us
    dot_general x1, matrix products, spectra_of(): jnp.dot(main, table, precision=lax.Precision.HIGH, preferred_element_type...  2.04 us

profile of v2, /device:TPU:1, one launch (start us, length us, event | category | flops | bytes accessed | tf_op | source)
XLA Modules:
  0.0 60.2 jit_solution(5195610420245927304)
XLA Ops:
  0.0 1.1 %pad_slice_fusion.2 = (f32[4,15]{1,0:T(4,128)S(1)}, f32[4,15]{1,0:T(4,128)S(1)}, f32[4,15]{1,0:T(4,128)S(1)}, f32[4,15]{1,0:T(4,128)S(1)}, f32[4,15]{1,0:T(4,128...) fusion(f32[4,16]{1,0:T(4,128)} %param.16), kind=kLoop, calls=%fused_computation.39 | loop fusion | bytes 6496 | tf_op jit(solution)/shard_map/slice | solution.py:61
  1.1 0.9 %pad_slice_fusion.3 = (f32[4,15]{1,0:T(4,128)S(1)}, f32[4,15]{1,0:T(4,128)S(1)}, f32[4,15]{1,0:T(4,128)S(1)}, f32[4,15]{1,0:T(4,128)S(1)}, f32[4,15]{1,0:T(4,128)S(1)}) fusion(f32[4,16]{1,0:T(4,128)} %param.16), kind=kLoop, calls=%fused_computation.40 | loop fusion | bytes 1456 | tf_op jit(solution)/shard_map/slice | solution.py:61
  2.1 0.1 stack.63
  2.1 0.0 copy-start.8
  2.2 0.0 copy-start.7
  2.2 1.8 %copy.82 = f32[4,16,4,2063]{3,1,0,2:T(8,128)S(1)} copy(f32[4,16,4,2063]{3,2,1,0:T(4,128)} %param.15) | data formatting | bytes 4225024 | tf_op args[0]
  4.0 0.2 convolution_bitcast_fusion.2
  4.2 0.0 copy-done.8
  4.2 0.3 fusion.16
  4.5 0.2 convolution_bitcast_fusion.1
  4.7 0.0 copy-done.7
  4.7 0.3 convolution_add_fusion
  5.1 0.3 slice.95
  5.4 2.7 %copy.83 = f32[64,4,2048]{2,1,0:T(4,128)} copy(f32[64,4,2048]{2,0,1:T(8,128)S(1)} %slice.95) | data formatting | bytes 4194304 | tf_op jit(solution)/shard_map/slice | solution.py:51
  8.0 3.0 %reshape.79 = f32[256,2048]{1,0:T(8,128)} reshape(f32[64,4,2048]{2,1,0:T(4,128)} %copy.83) | data formatting | bytes 4194304 | tf_op jit(solution)/shard_map/reshape | solution.py:51
  11.0 0.0 copy-done.2
  11.0 0.0 copy-done.3
  11.1 0.0 copy-done.5
  11.1 0.0 copy-done.6
  11.1 0.0 copy-start.1
  11.1 0.5 multiply_subtract_fusion
  11.5 0.0 copy-start
  11.5 1.3 %copy-done = f32[32,64,256]{2,1,0:T(8,128)} copy-done((f32[32,64,256]{2,1,0:T(8,128)}, f32[32,64,256]{2,1,0:T(8,128)S(1)}, u32[]{:S(2)}) %copy-start) | copy-done | bytes 2097176
  12.9 0.1 copy-done.1
  13.0 2.0 %fusion.5 = f32[256,512]{1,0:T(8,128)S(1)} fusion(f32[256,2048]{1,0:T(8,128)S(1)} %copy-done.1, f32[2048,256]{1,0:T(8,128)S(1)} %bitcast.91, f32[2048,256]{1,0:T(8,128)S(1)} %bitcast.89), kind=kOutput, calls=%fused_computation.10 | convolution fusion | flops 1611661312 | bytes 6815744 | tf_op jit(solution)/shard_map/dot_general | solution.py:52
  15.1 0.0 copy-start.13
  15.1 0.0 copy-start.12
  15.1 0.0 copy-start.14
  15.1 0.0 copy-start.9
  15.1 0.1 reshape.80
  15.3 0.0 copy-done.4
  15.3 0.0 copy-done.11
  15.3 0.1 convolution_bitcast_fusion.3
  15.4 0.0 copy-done.10
  15.4 0.1 convolution_bitcast_fusion.4
  15.6 0.4 subtract_reduce_fusion
  16.0 0.7 %pad_maximum_fusion.4.refs_0_ = f32[64,512]{1,0:T(8,128)} fusion(f32[64,256]{1,0:T(8,128)S(1)} %get-tuple-element.10, f32[64,256]{1,0:T(8,128)S(1)} %get-tuple-element.9), kind=kLoop, calls=%fused_computation.24 | loop fusion | flops 32768 | bytes 262144 | tf_op jit(solution)/shard_map/concatenate | solution.py:248
  16.7 0.1 copy.101
  16.8 0.1 fusion.7
  17.0 0.7 %reshape.90.refs_4_ = f32[128,1]{1,0:T(8,128)} reshape(f32[8,2,8]{2,1,0:T(2,128)S(1)} %copy.104) | data formatting | bytes 1024 | tf_op jit(solution)/shard_map/reshape | solution.py:207
  17.7 0.7 %convert_element_type.26.refs_1_ = f32[64,1]{1,0:T(8,128)} reshape(f32[4,16]{1,0:T(4,128)S(1)} %dynamic-slice_convert_fusion) | data formatting | bytes 512 | tf_op jit(solution)/shard_map/convert_element_type | solution.py:196
  18.4 0.0 copy-done.12
  18.4 0.2 convert_reduce_fusion
  18.6 0.7 %convolution_convert_fusion = bf16[128,128]{1,0:T(8,128)(2,1)} fusion(bf16[72,128]{1,0:T(8,128)(2,1)S(1)} %copy-done.9, s32[72]{0:T(128)S(1)} %multiply_add_fusion.1), kind=kOutput, calls=%fused_computation.12 | convolution fusion | flops 2384896 | bytes 51488 | tf_op jit(solution)/shard_map/dot_general | solution.py:223
  19.3 35.5 %combine.1 = bf16[64,8,128]{2,1,0:T(8,128)(2,1)} custom-call(f32[64,512]{1,0:T(8,128)} %pad_maximum_fusion.4.refs_0_, f32[64,1]{1,0:T(8,128)} %convert_element_type.26.refs_1_, f32[256,256]{1,0:T(8,128)} %constant.82.clone.refs_2_, f32[2,256]{1,0:T(2,128)} %constant.79.clone.refs_3_, f32[128,1]{1,0:T(8,128)} %reshape.90.refs_4_, bf16[2,64,128]{2,1,0:T(8,128)(2,1)} %bitcast.93), custom_call_target="tpu_custom_call" | custom-call | tf_op jit(solution)/shard_map/combine/pallas_call | solution.py:228
  54.8 1.0 %reshape.85 = bf16[64,2,512]{2,1,0:T(2,128)(2,1)S(1)} reshape(bf16[64,8,128]{2,1,0:T(8,128)(2,1)} %combine.1) | data formatting | bytes 262144 | tf_op jit(solution)/shard_map/reshape.35
  55.8 2.4 %convolution_bitcast_fusion = f32[1,64,2,1,2001]{4,1,2,3,0:T(8,128)S(1)} fusion(f32[2048,256]{1,0:T(8,128)} %bitcast.92, f32[2048,256]{1,0:T(8,128)S(1)} %bitcast.90, bf16[64,2,512]{2,1,0:T(2,128)(2,1)S(1)} %reshape.85), kind=kOutput, calls=%fused_computation.6 | convolution fusion | flops 266373120 | bytes 5349888 | tf_op jit(solution)/shard_map/dot_general | solution.py:250
  58.2 2.1 %copy.108 = f32[1,64,2,1,2001]{4,3,2,1,0:T(1,128)} copy(f32[1,64,2,1,2001]{4,1,2,3,0:T(8,128)S(1)} %convolution_bitcast_fusion) | data formatting | bytes 2049024 | tf_op jit(solution)/shard_map/dot_general | solution.py:250
  (17 shorter events, 0.1 us)
Async XLA Ops:
  2.1 2.0 %copy-start.8 = (f32[15,512]{1,0:T(8,128)S(1)}, f32[15,512]{1,0:T(8,128)}, u32[]{:S(2)}) copy-start(f32[15,512]{1,0:T(8,128)} %constant.92) | copy-start | bytes 92164
  2.2 2.6 %copy-start.7 = (f32[15,512]{1,0:T(8,128)S(1)}, f32[15,512]{1,0:T(8,128)}, u32[]{:S(2)}) copy-start(f32[15,512]{1,0:T(8,128)} %constant.93) | copy-start | bytes 92164
  8.0 3.0 %copy-start.2 = (f32[64,256]{1,0:T(8,128)S(1)}, f32[64,256]{1,0:T(8,128)}, u32[]{:S(2)}) copy-start(f32[64,256]{1,0:T(8,128)} %constant.89) | copy-start | bytes 196612
  8.0 3.0 %copy-start.3 = (f32[64,256]{1,0:T(8,128)S(1)}, f32[64,256]{1,0:T(8,128)}, u32[]{:S(2)}) copy-start(f32[64,256]{1,0:T(8,128)} %constant.91) | copy-start | bytes 196612
  8.0 3.0 %copy-start.5 = (f32[32,256]{1,0:T(8,128)S(1)}, f32[32,256]{1,0:T(8,128)}, u32[]{:S(2)}) copy-start(f32[32,256]{1,0:T(8,128)} %constant.88) | copy-start | bytes 98308
  8.0 3.0 %copy-start.6 = (f32[32,256]{1,0:T(8,128)S(1)}, f32[32,256]{1,0:T(8,128)}, u32[]{:S(2)}) copy-start(f32[32,256]{1,0:T(8,128)} %constant.90) | copy-start | bytes 98308
  11.1 1.9 %copy-start.1 = (f32[256,2048]{1,0:T(8,128)S(1)}, f32[256,2048]{1,0:T(8,128)}, u32[]{:S(2)}) copy-start(f32[256,2048]{1,0:T(8,128)} %reshape.79) | copy-start | bytes 6291460
  11.5 1.3 %copy-start = (f32[32,64,256]{2,1,0:T(8,128)}, f32[32,64,256]{2,1,0:T(8,128)S(1)}, u32[]{:S(2)}) copy-start(f32[32,64,256]{2,1,0:T(8,128)S(1)} %get-tuple-element.8) | copy-start | bytes 6291460
  13.0 2.3 %copy-start.4 = (f32[4,16]{1,0:T(4,128)S(1)}, f32[4,16]{1,0:T(4,128)}, u32[]{:S(2)}) copy-start(f32[4,16]{1,0:T(4,128)} %param.16) | copy-start | bytes 772
  13.0 2.3 %copy-start.11 = (f32[16,256]{1,0:T(8,128)S(1)}, f32[16,256]{1,0:T(8,128)}, u32[]{:S(2)}) copy-start(f32[16,256]{1,0:T(8,128)} %constant.77.clone) | copy-start | bytes 49156
  13.0 2.4 %copy-start.10 = (f32[16,256]{1,0:T(8,128)S(1)}, f32[16,256]{1,0:T(8,128)}, u32[]{:S(2)}) copy-start(f32[16,256]{1,0:T(8,128)} %constant.76.clone) | copy-start | bytes 49156
  15.1 1.6 %copy-start.13 = (s32[32,16]{0,1:T(8,128)S(1)}, s32[32,16]{0,1:T(8,128)}, u32[]{:S(2)}) copy-start(s32[32,16]{0,1:T(8,128)} %param.17) | copy-start | bytes 6148
  15.1 3.3 %copy-start.12 = (pred[72,72]{1,0:T(8,128)(4,1)S(1)}, pred[72,72]{1,0:T(8,128)(4,1)}, u32[]{:S(2)}) copy-start(pred[72,72]{1,0:T(8,128)(4,1)} %constant.80.clone) | copy-start | bytes 15556
  15.1 3.3 %copy-start.14 = (s32[1,72,1]{1,2,0:T(1,128)S(1)}, s32[1,72,1]{1,2,0:T(1,128)}, u32[]{:S(2)}) copy-start(s32[1,72,1]{1,2,0:T(1,128)} %param.18) | copy-start | bytes 868
  15.1 3.5 %copy-start.9 = (bf16[72,128]{1,0:T(8,128)(2,1)S(1)}, bf16[72,128]{1,0:T(8,128)(2,1)}, u32[]{:S(2)}) copy-start(bf16[72,128]{1,0:T(8,128)(2,1)} %constant.81.clone) | copy-start | bytes 55300

commit v3 on v2

v3 whole, which is shorter than its diff:
```python
import functools
import math

import jax
import jax.numpy as jnp
import numpy as np
from jax import lax
from jax.experimental import pallas as pl
from jax.experimental.pallas import tpu as pltpu
from jax.sharding import PartitionSpec as P

SEG = 2048
NB = 256
K0 = 16
SMOOTH = 32
MAXLAG = 1000
CAP = 2
SPLIT = 2
STEP = 64

EPSILON = 1e-06
PRECISE = lax.Precision.HIGHEST
FREQS = K0 + np.arange(NB)


def turn(multiples):
    angle = (np.asarray(multiples)[:, None] * FREQS[None, :] % (2 * SEG)) * (math.pi / SEG)
    return np.cos(angle).astype(np.float32), (-np.sin(angle)).astype(np.float32)


def wave_steps():
    coarse = np.concatenate(turn(STEP * np.arange(SEG // STEP)), axis=1)
    fine = np.concatenate(turn(np.arange(STEP)), axis=1)
    return coarse, fine


def smoother():
    near = np.abs(np.arange(NB)[:, None] - np.arange(NB)[None, :]) <= SMOOTH
    return near.astype(np.float32) / (2 * SMOOTH + 1)


def edge_waves(taps):
    adv = np.concatenate(turn(-np.arange(taps)), axis=1)
    sign = np.where(FREQS % 2 == 0, 1.0, -1.0).astype(np.float32)
    edges = np.zeros((128, 2 * NB), np.float32)
    for j in range(1, taps):
        edges[128 - j] = -adv[j]
        edges[64 - j] = adv[j] * np.concatenate([sign, sign])
    return adv, edges


def pair_spread(members):
    rows_of, cols_of = np.triu_indices(members)
    pair_i = np.repeat(rows_of, SPLIT)
    pair_j = np.repeat(cols_of, SPLIT)
    pair_h = np.tile(np.arange(SPLIT), rows_of.shape[0])
    combo_of = (pair_i * SPLIT + pair_h) * members + pair_j
    spread = np.zeros((combo_of.size, members * SPLIT * members), np.float32)
    spread[np.arange(combo_of.size), combo_of] = 1.0
    return spread


def ints(shape, axis):
    return lax.broadcasted_iota(jnp.int32, shape, axis)


def exact_dot(a, b):
    return jnp.dot(a, b, precision=PRECISE, preferred_element_type=jnp.float32)


def combine(members, groups, stations, windows, phases, *refs):
    (raw_hbm, ends_ref, taps_ref, valid_ref, owners_ref) = refs[:5]
    (coarse_ref, fine_ref, adv_ref, edge_ref, smooth_ref, lead_ref, spread_ref) = refs[5:12]
    out_ref, waves = refs[12:14]
    (raw, rest, whole, white, left, right, stack, held, staged, routed, arrived) = refs[14:25]
    raw_sem, near_send, near_recv, far_send, far_recv = refs[25:]
    mine = lax.axis_index("sta")
    group = lax.axis_index("grp")
    half = stations // SPLIT
    rows = stations * windows

    load = pltpu.make_async_copy(raw_hbm, raw, raw_sem)
    load.start()
    barrier = pltpu.get_barrier_semaphore()

    @pl.loop(1, groups)
    def _(k):
        pl.semaphore_signal(
            barrier,
            inc=1,
            device_id={"grp": lax.rem(group + k, groups)},
            device_id_type=pl.DeviceIdType.MESH,
        )

    @pl.loop(1, members)
    def _(k):
        pl.semaphore_signal(
            barrier,
            inc=1,
            device_id={"sta": lax.rem(mine + k, members)},
            device_id_type=pl.DeviceIdType.MESH,
        )

    @pl.loop(0, SEG // STEP)
    def _(step):
        at = pl.ds(pl.multiple_of(step * STEP, STEP), STEP)
        cr, ci = coarse_ref[pl.ds(step, 1), :NB], coarse_ref[pl.ds(step, 1), NB:]
        fr, fi = fine_ref[:, :NB], fine_ref[:, NB:]
        for part, wave in enumerate((cr * fr - ci * fi, cr * fi + ci * fr)):
            upper = wave.astype(jnp.bfloat16)
            waves[at, part * NB : (part + 1) * NB] = upper
            lower = (wave - upper.astype(jnp.float32)).astype(jnp.bfloat16)
            rest[at, part * NB : (part + 1) * NB] = lower

    phase_taps = taps_ref[...]
    gains = exact_dot(phase_taps, adv_ref[...])
    ends = ends_ref[...]
    past = ends * phase_taps[:, 0:1]
    for q in range(1, phase_taps.shape[1]):
        past = past + pltpu.roll(ends, 128 - q, 1) * phase_taps[:, q : q + 1]
    fix = exact_dot(past, edge_ref[...])
    valid = valid_ref[...].astype(jnp.float32)
    wide = valid.shape[0]
    pick = ints((rows, wide), 1) == mine * stations + ints((rows, wide), 0) // windows
    own = exact_dot(pick.astype(jnp.float32), valid)
    here = ints(own.shape, 1) == lax.rem(ints(own.shape, 0), windows)
    own = jnp.sum(jnp.where(here, own, 0.0), axis=1, keepdims=True)
    sides = members * SPLIT
    pick = ints((sides, wide), 1) == half * ints((sides, wide), 0) + mine // stations
    held[...] = exact_dot(pick.astype(jnp.float32), valid)
    pick = ints((members, wide), 1) == stations * ints((members, wide), 0) + lax.rem(mine, stations)
    valid_right = exact_dot(pick.astype(jnp.float32), valid)
    owners = owners_ref[...]
    blocks = owners.shape[1]
    owned = (ints((groups, blocks), 0) == owners).astype(jnp.float32)
    earlier = (ints((blocks, blocks), 0) < ints((blocks, blocks), 1)).astype(jnp.float32)
    rank = exact_dot(owned, earlier)
    ontos = []
    for slot in range(CAP):
        chosen = jnp.where(jnp.abs(rank - slot) < 0.5, owned, 0.0)
        onto = jnp.dot(
            chosen.astype(jnp.bfloat16), spread_ref[...], preferred_element_type=jnp.float32
        )
        ontos.append(onto.astype(jnp.bfloat16))

    whole[...] = jnp.zeros_like(whole)
    load.wait()

    @pl.loop(0, SEG // NB)
    def _(step):
        at = pl.ds(pl.multiple_of(step * NB, NB), NB)
        block = raw[:, :, at].reshape(rows * phases, NB)
        upper = block.astype(jnp.bfloat16)
        lower = (block - upper.astype(jnp.float32)).astype(jnp.bfloat16)
        table = waves[at, :]
        total = jnp.dot(upper, table, preferred_element_type=jnp.float32)
        total = total + jnp.dot(upper, rest[at, :], preferred_element_type=jnp.float32)
        total = total + jnp.dot(lower, table, preferred_element_type=jnp.float32)
        whole[...] += total

    whole_re, whole_im = whole[:, :NB], whole[:, NB:]
    gain_re, gain_im = gains[:, :NB], gains[:, NB:]
    join = (ints((rows, rows * phases), 1) // phases == ints((rows, rows * phases), 0)).astype(jnp.float32)
    real = exact_dot(join, whole_re * gain_re - whole_im * gain_im + fix[:, :NB])
    imag = exact_dot(join, whole_re * gain_im + whole_im * gain_re + fix[:, NB:])
    smoothed = exact_dot(real * real + imag * imag, smooth_ref[...])
    whitener = own / jnp.sqrt(smoothed + EPSILON)
    white[:, :, :NB] = (real * whitener).astype(jnp.bfloat16).reshape(stations, windows, NB)
    white[:, :, NB:] = (imag * whitener).astype(jnp.bfloat16).reshape(stations, windows, NB)

    def near(k):
        peer = lax.rem(mine + k, members)
        side_a, side_c = peer // stations, lax.rem(peer, stations)
        copies = []
        for part in range(SPLIT + 1):
            station = side_c if part == SPLIT else part * half + side_a
            into = right.at[mine] if part == SPLIT else left.at[mine, part]
            copies.append(
                pltpu.make_async_remote_copy(
                    src_ref=white.at[station],
                    dst_ref=into,
                    send_sem=near_send.at[k, part],
                    recv_sem=near_recv.at[k, part],
                    device_id={"sta": peer},
                    device_id_type=pl.DeviceIdType.MESH,
                )
            )
        return copies

    pl.semaphore_wait(barrier, members - 1 + groups - 1)
    for k in range(1, members):
        for copy in near(k):
            copy.start()
    for part in range(SPLIT):
        left[mine, part] = white[part * half + mine // stations]
    right[mine] = white[lax.rem(mine, stations)]
    for k in range(1, members):
        for copy in near(k):
            copy.wait()

    @pl.loop(0, members * SPLIT)
    def _(n):
        i, h = n // SPLIT, lax.rem(n, SPLIT)
        ours = left[i, h].astype(jnp.float32)
        theirs = right[...].astype(jnp.float32)
        lr, li = ours[None, :, :NB], ours[None, :, NB:]
        rr, ri = theirs[:, :, :NB], theirs[:, :, NB:]
        rows = pl.ds(pl.multiple_of(n * members, members), members)
        count = jnp.sum(held[pl.ds(n, 1), :] * valid_right, axis=1, keepdims=True)
        scale = 1.0 / (math.sqrt(NB) * jnp.maximum(count, 1.0))
        stack[rows, :NB] = jnp.sum(lr * rr + li * ri, axis=1) * scale
        stack[rows, NB:] = jnp.sum(li * rr - lr * ri, axis=1) * scale

    lead_re, lead_im = lead_ref[0:1], lead_ref[1:2]
    stack_re, stack_im = stack[:, :NB], stack[:, NB:]
    moved_re = (stack_re * lead_re - stack_im * lead_im).astype(jnp.bfloat16)
    moved_im = (stack_re * lead_im + stack_im * lead_re).astype(jnp.bfloat16)
    for slot in range(CAP):
        for part, moved in enumerate((moved_re, moved_im)):
            placed = jnp.dot(ontos[slot], moved, preferred_element_type=jnp.float32)
            for chunk in range(NB // 128):
                row = slot * (2 * NB // 128) + part * (NB // 128) + chunk
                staged[:, row, :] = placed[:, chunk * 128 : (chunk + 1) * 128]
    routed[...] = staged[...].astype(jnp.bfloat16)

    def far(k):
        peer = lax.rem(group + k, groups)
        return pltpu.make_async_remote_copy(
            src_ref=routed.at[peer],
            dst_ref=arrived.at[group],
            send_sem=far_send.at[k],
            recv_sem=far_recv.at[k],
            device_id={"grp": peer},
            device_id_type=pl.DeviceIdType.MESH,
        )

    @pl.loop(1, groups)
    def _(k):
        far(k).start()

    arrived[group] = routed[group]

    @pl.loop(1, groups)
    def _(k):
        far(k).wait()

    out_ref[...] = arrived[...]


def local(seismograms, fir_taps, valid_windows, pair_owners):
    stations, windows, phases, samples = seismograms.shape
    members = lax.axis_size("sta")
    groups = lax.axis_size("grp")
    taps = fir_taps.shape[1]
    rows = stations * windows
    combos = members * SPLIT * members
    raw = seismograms.reshape(rows, phases, samples)
    spare = jnp.zeros((stations, windows, phases, 64 - (taps - 1)), jnp.float32)
    head, tail = seismograms[..., : taps - 1], seismograms[..., SEG:]
    ends = jnp.concatenate([head, spare, tail, spare], axis=-1).reshape(rows * phases, 128)
    phase_taps = jnp.tile(fir_taps, (rows, 1))
    coarse, fine = wave_steps()
    adv, edges = edge_waves(taps)
    lead = np.concatenate(turn([MAXLAG]))
    spread = jnp.asarray(pair_spread(members), jnp.bfloat16)

    vmem = pl.BlockSpec(memory_space=pltpu.VMEM)
    tile = (groups, CAP * 2 * NB // 128, 128)
    arrived, waves = pl.pallas_call(
        functools.partial(combine, members, groups, stations, windows, phases),
        out_shape=(
            jax.ShapeDtypeStruct(tile, jnp.bfloat16),
            jax.ShapeDtypeStruct((SEG, 2 * NB), jnp.bfloat16),
        ),
        in_specs=[pl.BlockSpec(memory_space=pl.ANY)] + [vmem] * 11,
        out_specs=(vmem, vmem),
        scratch_shapes=[
            pltpu.VMEM((rows, phases, samples), jnp.float32),
            pltpu.VMEM((SEG, 2 * NB), jnp.bfloat16),
            pltpu.VMEM((rows * phases, 2 * NB), jnp.float32),
            pltpu.VMEM((stations, windows, 2 * NB), jnp.bfloat16),
            pltpu.VMEM((members, SPLIT, windows, 2 * NB), jnp.bfloat16),
            pltpu.VMEM((members, windows, 2 * NB), jnp.bfloat16),
            pltpu.VMEM((combos, 2 * NB), jnp.float32),
            pltpu.VMEM((members * SPLIT, windows), jnp.float32),
            pltpu.VMEM(tile, jnp.float32),
            pltpu.VMEM(tile, jnp.bfloat16),
            pltpu.VMEM(tile, jnp.bfloat16),
            pltpu.SemaphoreType.DMA,
            pltpu.SemaphoreType.DMA((members, SPLIT + 1)),
            pltpu.SemaphoreType.DMA((members, SPLIT + 1)),
            pltpu.SemaphoreType.DMA((groups,)),
            pltpu.SemaphoreType.DMA((groups,)),
        ],
        compiler_params=pltpu.CompilerParams(collective_id=0, has_side_effects=True),
        name="combine",
    )(
        raw,
        ends,
        phase_taps,
        valid_windows,
        pair_owners.reshape(1, -1),
        coarse,
        fine,
        adv,
        edges,
        smoother(),
        lead,
        spread,
    )
    lagged = lax.dot_general(
        arrived.reshape(groups * CAP, 2 * NB),
        waves[: 2 * MAXLAG + 1],
        (((1,), (1,)), ((), ())),
        preferred_element_type=jnp.float32,
    )
    return lagged.reshape(1, groups, CAP, 1, 2 * MAXLAG + 1)


def solution(mesh):
    in_specs = (P(("grp", "sta"), None, None, None), P(), P("grp", None), P("grp", None, None))
    out_specs = P("grp", None, None, "sta", None)
    return jax.shard_map(local, mesh=mesh, in_specs=in_specs, out_specs=out_specs, check_vma=False)
```

time: 60.6 us -> 52.1 us (0.86)
  local copies, waits for them, and re-layouts: 16.1 us -> 6.75 us
  Pallas kernels: 35.5 us -> 41.7 us
  matrix products: 6.6 us -> 2.37 us
  other arithmetic: 1.74 us -> 0.93 us
    pallas_call x1, Pallas kernels: 35.5 us -> 41.7 us  [local(): pl.pallas_call(functools.partial(combine, members, groups, stations, wind...]
    dot_general x10 -> x1, matrix products: 6.6 us -> 2.37 us  [local(): lax.dot_general(arrived.reshape(groups * CAP, 2 * NB), waves[:2 * MAXLAG...]
    slice x4 -> x1, local copies, waits for them, and re-layouts: 5.01 us -> 0.99 us  [local(): head, tail = (seismograms[..., :taps - 1], seismograms[..., SEG:])]
    reshape x3 -> x0, local copies, waits for them, and re-layouts: 3.86 us -> none  [the longest x1 3 us: spectra_of(): main = raw[:, :, :SEG].reshape(rows * phases, SEG)]
    unnamed x32 -> x1, local copies, waits for them, and re-layouts: 3.44 us -> 1.37 us
    another operation x2, local copies, waits for them, and re-layouts: 1.03 us -> 2.32 us  [the longest x1 1.36 us: local(): phase_taps = jnp.tile(fir_taps, (rows, 1))]
    convert_element_type x1 -> x0, local copies, waits for them, and re-layouts: 0.69 us -> none  [local(): own_valid = own_valid.reshape(-1, 1).astype(jnp.float32)]
where the time goes in v3:
time: 52.1 us; the launch traced here: 51.8 us
  Pallas kernels  41.7 us (80%)
  local copies, waits for them, and re-layouts  6.75 us (13%)
  matrix products  2.37 us (5%)
  other arithmetic  0.93 us (2%)
    pallas_call x1, Pallas kernels, local(): pl.pallas_call(functools.partial(combine, members, groups, stations, wind...  41.7 us
    dot_general x1, matrix products, local(): lax.dot_general(arrived.reshape(groups * CAP, 2 * NB), waves[:2 * MAXLAG...  2.37 us
    dot_general x1, local copies, waits for them, and re-layouts, local(): lax.dot_general(arrived.reshape(groups * CAP, 2 * NB), waves[:2 * MAXLAG...  2.05 us
    unnamed x1, local copies, waits for them, and re-layouts  1.37 us
    another operation x1, local copies, waits for them, and re-layouts, local(): phase_taps = jnp.tile(fir_taps, (rows, 1))  1.36 us

profile of v3, /device:TPU:1, one launch (start us, length us, event | category | flops | bytes accessed | tf_op | source)
XLA Modules:
  0.0 51.8 jit_solution(3406929756344196661)
XLA Ops:
  0.0 1.4 %copy.12.refs_3_ = s32[32,16]{1,0:T(8,128)} copy(s32[32,16]{0,1:T(8,128)} %param.13) | data formatting | bytes 4096 | tf_op args[2]
  1.4 1.4 %tile.4 = f32[64,4,16]{2,1,0:T(4,128)} broadcast(f32[4,16]{1,0:T(4,128)} %param.12), dimensions={1,2} | broadcast | bytes 16640 | tf_op jit(solution)/shard_map/tile | solution.py:261
  2.7 1.0 %fusion.3 = (f32[4,16,4,15]{3,2,1,0:T(4,128)S(1)}, f32[4,16,4,15]{3,2,1,0:T(4,128)S(1)}) fusion(f32[4,16,4,2063]{3,2,1,0:T(4,128)} %param.11), kind=kLoop, calls=%fused_computation.5 | loop fusion | bytes 61440 | tf_op jit(solution)/shard_map/slice | solution.py:259
  3.7 0.9 %pad_maximum_fusion = f32[4,16,4,128]{3,2,1,0:T(4,128)} fusion(f32[4,16,4,49]{3,2,1,0:T(4,128)S(1)} %broadcast_in_dim.3, f32[4,16,4,15]{3,2,1,0:T(4,128)S(1)} %get-tuple-element.10, f32[4,16,4,15]{3,2,1,0:T(4,128)S(1)} %get-tuple-element.9), kind=kLoop, calls=%fused_computation.3 | loop fusion | flops 98304 | bytes 211968 | tf_op jit(solution)/shard_map/concatenate | solution.py:260
  4.7 41.7 %combine.1 = (bf16[64,8,128]{2,1,0:T(8,128)(2,1)}, bf16[2048,512]{1,0:T(8,128)(2,1)}) custom-call(f32[64,4,2063]{2,1,0:T(4,128)} %bitcast.9, f32[256,128]{1,0:T(8,128)} %bitcast.11, f32[256,16]{1,0:T(8,128)} %bitcast.10, s32[32,16]{1,0:T(8,128)} %copy.12.refs_3_, s32[1,72]{1,0:T(1,128)} %bitcast.12, f32[32,512]{1,0:T(8,128)} %constant.17.clone.refs_5_, ...), custom_call_target="tpu_custom_call" | custom-call | tf_op jit(solution)/shard_map/combine/pallas_call | solution.py:269
  46.4 1.0 %reshape.28 = bf16[64,2,512]{2,1,0:T(2,128)(2,1)S(1)} reshape(bf16[64,8,128]{2,1,0:T(8,128)(2,1)} %get-tuple-element.7) | data formatting | bytes 262144 | tf_op jit(solution)/shard_map/reshape.12
  47.4 2.4 %convolution_bitcast_fusion = f32[1,64,2,1,2001]{4,1,2,3,0:T(8,128)S(1)} fusion(bf16[2048,512]{1,0:T(8,128)(2,1)} %get-tuple-element.8, bf16[64,2,512]{2,1,0:T(2,128)(2,1)S(1)} %reshape.28), kind=kOutput, calls=%fused_computation | convolution fusion | flops 262275072 | bytes 3211776 | tf_op jit(solution)/shard_map/dot_general | solution.py:311
  49.8 2.1 %copy.14 = f32[1,64,2,1,2001]{4,3,2,1,0:T(1,128)} copy(f32[1,64,2,1,2001]{4,1,2,3,0:T(8,128)S(1)} %convolution_bitcast_fusion) | data formatting | bytes 2049024 | tf_op jit(solution)/shard_map/dot_general | solution.py:311
  (1 shorter events, 0.0 us)

commit v4 on v3

--- a/solution.py
+++ b/solution.py
@@ -68,12 +68,18 @@
     return jnp.dot(a, b, precision=PRECISE, preferred_element_type=jnp.float32)
 
 
+def exact_dot_t(a, b):
+    return lax.dot_general(
+        a, b, (((1,), (1,)), ((), ())), precision=PRECISE, preferred_element_type=jnp.float32
+    )
+
+
 def combine(members, groups, stations, windows, phases, *refs):
-    (raw_hbm, ends_ref, taps_ref, valid_ref, owners_ref) = refs[:5]
-    (coarse_ref, fine_ref, adv_ref, edge_ref, smooth_ref, lead_ref, spread_ref) = refs[5:12]
-    out_ref, waves = refs[12:14]
-    (raw, rest, whole, white, left, right, stack, held, staged, routed, arrived) = refs[14:25]
-    raw_sem, near_send, near_recv, far_send, far_recv = refs[25:]
+    (raw_hbm, taps_ref, valid_ref, owners_ref) = refs[:4]
+    (coarse_ref, fine_ref, adv_ref, edge_ref, smooth_ref, lead_ref, spread_ref) = refs[4:11]
+    out_ref = refs[11]
+    (raw, waves, rest, whole, white, left, right, stack, held, staged, routed, arrived) = refs[12:24]
+    raw_sem, near_send, near_recv, far_send, far_recv = refs[24:]
     mine = lax.axis_index("sta")
     group = lax.axis_index("grp")
     half = stations // SPLIT
@@ -83,7 +89,7 @@
     load.start()
     barrier = pltpu.get_barrier_semaphore()
 
-    @pl.loop(1, groups)
+    @pl.loop(1, groups, unroll=7)
     def _(k):
         pl.semaphore_signal(
             barrier,
@@ -112,24 +118,21 @@
             lower = (wave - upper.astype(jnp.float32)).astype(jnp.bfloat16)
             rest[at, part * NB : (part + 1) * NB] = lower
 
-    phase_taps = taps_ref[...]
+    pick = ints((rows * phases, phases), 1) == lax.rem(ints((rows * phases, phases), 0), phases)
+    phase_taps = exact_dot(pick.astype(jnp.float32), taps_ref[...])
+    taps = phase_taps.shape[1]
     gains = exact_dot(phase_taps, adv_ref[...])
-    ends = ends_ref[...]
-    past = ends * phase_taps[:, 0:1]
-    for q in range(1, phase_taps.shape[1]):
-        past = past + pltpu.roll(ends, 128 - q, 1) * phase_taps[:, q : q + 1]
-    fix = exact_dot(past, edge_ref[...])
     valid = valid_ref[...].astype(jnp.float32)
-    wide = valid.shape[0]
+    wide = valid.shape[1]
     pick = ints((rows, wide), 1) == mine * stations + ints((rows, wide), 0) // windows
-    own = exact_dot(pick.astype(jnp.float32), valid)
+    own = exact_dot_t(pick.astype(jnp.float32), valid)
     here = ints(own.shape, 1) == lax.rem(ints(own.shape, 0), windows)
     own = jnp.sum(jnp.where(here, own, 0.0), axis=1, keepdims=True)
     sides = members * SPLIT
     pick = ints((sides, wide), 1) == half * ints((sides, wide), 0) + mine // stations
-    held[...] = exact_dot(pick.astype(jnp.float32), valid)
+    held[...] = exact_dot_t(pick.astype(jnp.float32), valid)
     pick = ints((members, wide), 1) == stations * ints((members, wide), 0) + lax.rem(mine, stations)
-    valid_right = exact_dot(pick.astype(jnp.float32), valid)
+    valid_right = exact_dot_t(pick.astype(jnp.float32), valid)
     owners = owners_ref[...]
     blocks = owners.shape[1]
     owned = (ints((groups, blocks), 0) == owners).astype(jnp.float32)
@@ -143,8 +146,17 @@
         )
         ontos.append(onto.astype(jnp.bfloat16))
 
+    load.wait()
+    lanes = ints((rows * phases, 128), 1)
+    head = raw[:, :, :128].reshape(rows * phases, 128)
+    tail = raw[:, :, SEG + taps - 1 - 128 :].reshape(rows * phases, 128)
+    tail = pltpu.roll(jnp.where(lanes > 128 - taps, tail, 0.0), 64 + taps - 1, 1)
+    ends = jnp.where(lanes < taps - 1, head, tail)
+    past = ends * phase_taps[:, 0:1]
+    for q in range(1, taps):
+        past = past + pltpu.roll(ends, 128 - q, 1) * phase_taps[:, q : q + 1]
+    fix = exact_dot(past, edge_ref[...])
     whole[...] = jnp.zeros_like(whole)
-    load.wait()
 
     @pl.loop(0, SEG // NB)
     def _(step):
@@ -198,7 +210,7 @@
         for copy in near(k):
             copy.wait()
 
-    @pl.loop(0, members * SPLIT)
+    @pl.loop(0, members * SPLIT, unroll=4)
     def _(n):
         i, h = n // SPLIT, lax.rem(n, SPLIT)
         ours = left[i, h].astype(jnp.float32)
@@ -234,17 +246,48 @@
             device_id_type=pl.DeviceIdType.MESH,
         )
 
-    @pl.loop(1, groups)
+    @pl.loop(1, groups, unroll=7)
     def _(k):
         far(k).start()
 
     arrived[group] = routed[group]
 
-    @pl.loop(1, groups)
+    @pl.loop(1, groups, unroll=7)
     def _(k):
         far(k).wait()
 
     out_ref[...] = arrived[...]
+
+
+def to_lags(arrived_ref, coarse_ref, fine_ref, out_ref, staged):
+    staged[...] = arrived_ref[...].astype(jnp.float32)
+    chunks = 2 * NB // 128
+    sides = []
+    for slot in range(CAP):
+        parts = [staged[:, slot * chunks + c, :] for c in range(chunks)]
+        sides.append(jnp.concatenate(parts, axis=1))
+    stacks = jnp.concatenate(sides, axis=0).astype(jnp.bfloat16)
+    groups = arrived_ref.shape[0]
+    fr, fi = fine_ref[:, :NB], fine_ref[:, NB:]
+    lags = out_ref.shape[-1]
+    wide = 2 * STEP
+    for first in range(0, lags, wide):
+        real, imag = [], []
+        for step in range(first // STEP, (first + wide) // STEP):
+            cr, ci = coarse_ref[step : step + 1, :NB], coarse_ref[step : step + 1, NB:]
+            real.append((cr * fr - ci * fi).astype(jnp.bfloat16))
+            imag.append((cr * fi + ci * fr).astype(jnp.bfloat16))
+        table = jnp.concatenate(
+            [jnp.concatenate(real, axis=0), jnp.concatenate(imag, axis=0)], axis=1
+        )
+        block = lax.dot_general(
+            stacks, table, (((1,), (1,)), ((), ())), preferred_element_type=jnp.float32
+        )
+        width = min(wide, lags - first)
+        for slot in range(CAP):
+            out_ref[:, slot, 0, first : first + width] = block[
+                slot * groups : (slot + 1) * groups, :width
+            ]
 
 
 def local(seismograms, fir_taps, valid_windows, pair_owners):
@@ -255,10 +298,6 @@
     rows = stations * windows
     combos = members * SPLIT * members
     raw = seismograms.reshape(rows, phases, samples)
-    spare = jnp.zeros((stations, windows, phases, 64 - (taps - 1)), jnp.float32)
-    head, tail = seismograms[..., : taps - 1], seismograms[..., SEG:]
-    ends = jnp.concatenate([head, spare, tail, spare], axis=-1).reshape(rows * phases, 128)
-    phase_taps = jnp.tile(fir_taps, (rows, 1))
     coarse, fine = wave_steps()
     adv, edges = edge_waves(taps)
     lead = np.concatenate(turn([MAXLAG]))
@@ -266,16 +305,14 @@
 
     vmem = pl.BlockSpec(memory_space=pltpu.VMEM)
     tile = (groups, CAP * 2 * NB // 128, 128)
-    arrived, waves = pl.pallas_call(
+    arrived = pl.pallas_call(
         functools.partial(combine, members, groups, stations, windows, phases),
-        out_shape=(
-            jax.ShapeDtypeStruct(tile, jnp.bfloat16),
-            jax.ShapeDtypeStruct((SEG, 2 * NB), jnp.bfloat16),
-        ),
-        in_specs=[pl.BlockSpec(memory_space=pl.ANY)] + [vmem] * 11,
-        out_specs=(vmem, vmem),
+        out_shape=jax.ShapeDtypeStruct(tile, jnp.bfloat16),
+        in_specs=[pl.BlockSpec(memory_space=pl.ANY)] + [vmem] * 10,
+        out_specs=vmem,
         scratch_shapes=[
             pltpu.VMEM((rows, phases, samples), jnp.float32),
+            pltpu.VMEM((SEG, 2 * NB), jnp.bfloat16),
             pltpu.VMEM((SEG, 2 * NB), jnp.bfloat16),
             pltpu.VMEM((rows * phases, 2 * NB), jnp.float32),
             pltpu.VMEM((stations, windows, 2 * NB), jnp.bfloat16),
@@ -296,9 +333,8 @@
         name="combine",
     )(
         raw,
-        ends,
-        phase_taps,
-        valid_windows,
+        fir_taps,
+        valid_windows.T,
         pair_owners.reshape(1, -1),
         coarse,
         fine,
@@ -308,13 +344,15 @@
         lead,
         spread,
     )
-    lagged = lax.dot_general(
-        arrived.reshape(groups * CAP, 2 * NB),
-        waves[: 2 * MAXLAG + 1],
-        (((1,), (1,)), ((), ())),
-        preferred_element_type=jnp.float32,
-    )
-    return lagged.reshape(1, groups, CAP, 1, 2 * MAXLAG + 1)
+    lagged = pl.pallas_call(
+        to_lags,
+        out_shape=jax.ShapeDtypeStruct((groups, CAP, 1, 2 * MAXLAG + 1), jnp.float32),
+        in_specs=[vmem] * 3,
+        out_specs=vmem,
+        scratch_shapes=[pltpu.VMEM(tile, jnp.float32)],
+        name="to_lags",
+    )(arrived, coarse, fine)
+    return lagged[None, :, :, :, :]
 
 
 def solution(mesh):

time: 52.1 us -> 44.9 us (0.86)
  local copies, waits for them, and re-layouts: 6.75 us -> 0 us
  Pallas kernels: 41.7 us -> 44.8 us
  matrix products: 2.37 us -> 0 us
  other arithmetic: 0.93 us -> 0 us
    pallas_call x0 -> x1, Pallas kernels: none -> 3.45 us  [local(): pl.pallas_call(to_lags, out_shape=jax.ShapeDtypeStruct((groups, CAP, 1, 2...]
    dot_general x1 -> x0, matrix products: 2.37 us -> none  [local(): lax.dot_general(arrived.reshape(groups * CAP, 2 * NB), waves[:2 * MAXLAG...]
    another operation x2 -> x0, local copies, waits for them, and re-layouts: 2.32 us -> none  [the longest x1 1.36 us: local(): phase_taps = jnp.tile(fir_taps, (rows, 1))]
    dot_general x1 -> x0, local copies, waits for them, and re-layouts: 2.05 us -> none  [local(): lax.dot_general(arrived.reshape(groups * CAP, 2 * NB), waves[:2 * MAXLAG...]
    unnamed x1 -> x0, local copies, waits for them, and re-layouts: 1.37 us -> none
    slice x1 -> x0, local copies, waits for them, and re-layouts: 0.99 us -> none  [local(): head, tail = (seismograms[..., :taps - 1], seismograms[..., SEG:])]
    concatenate x1 -> x0, other arithmetic: 0.93 us -> none  [local(): jnp.concatenate([head, spare, tail, spare], axis=-1)]
where the time goes in v4:
time: 44.9 us; the launch traced here: 44.8 us
  Pallas kernels  44.8 us (100%)
    pallas_call x1, Pallas kernels, local(): pl.pallas_call(functools.partial(combine, members, groups, stations, wind...  41.3 us
    pallas_call x1, Pallas kernels, local(): pl.pallas_call(to_lags, out_shape=jax.ShapeDtypeStruct((groups, CAP, 1, 2...  3.45 us

profile of v4, /device:TPU:1, one launch (start us, length us, event | category | flops | bytes accessed | tf_op | source)
XLA Modules:
  0.0 44.8 jit_solution(3577741561316249981)
XLA Ops:
  0.0 41.3 %combine.1.arrived_ref = bf16[64,8,128]{2,1,0:T(8,128)(2,1)} custom-call(f32[64,4,2063]{2,1,0:T(4,128)} %bitcast.4, f32[4,16]{1,0:T(4,128)} %refs_1_.1, s32[16,32]{1,0:T(8,128)} %bitcast.5, s32[1,72]{1,0:T(1,128)} %bitcast.6, f32[32,512]{1,0:T(8,128)} %constant.15.clone.refs_4_.coarse_ref, f32[64,512]{1,0:T(8,128)} %constant.16.clone.refs_5_.fine_ref, ...), custom_call_target="tpu_custom_call" | custom-call | tf_op jit(solution)/shard_map/combine/pallas_call | solution.py:308
  41.3 3.4 %to_lags.1 = f32[64,2,1,2001]{3,2,1,0:T(1,128)} custom-call(bf16[64,8,128]{2,1,0:T(8,128)(2,1)} %combine.1.arrived_ref, f32[32,512]{1,0:T(8,128)} %constant.15.clone.refs_4_.coarse_ref, f32[64,512]{1,0:T(8,128)} %constant.16.clone.refs_5_.fine_ref), custom_call_target="tpu_custom_call" | custom-call | tf_op jit(solution)/shard_map/to_lags/pallas_call | solution.py:347

commit v5 on v4

--- a/solution.py
+++ b/solution.py
@@ -17,6 +17,7 @@
 CAP = 2
 SPLIT = 2
 STEP = 64
+INNER = 8
 
 EPSILON = 1e-06
 PRECISE = lax.Precision.HIGHEST
@@ -78,8 +79,8 @@
     (raw_hbm, taps_ref, valid_ref, owners_ref) = refs[:4]
     (coarse_ref, fine_ref, adv_ref, edge_ref, smooth_ref, lead_ref, spread_ref) = refs[4:11]
     out_ref = refs[11]
-    (raw, waves, rest, whole, white, left, right, stack, held, staged, routed, arrived) = refs[12:24]
-    raw_sem, near_send, near_recv, far_send, far_recv = refs[24:]
+    (raw, waves, rest, whole, white, left, right, stack, held, staged, routed) = refs[12:23]
+    passing, arrived, raw_sem, near_send, near_recv, far_send, far_recv = refs[23:]
     mine = lax.axis_index("sta")
     group = lax.axis_index("grp")
     half = stations // SPLIT
@@ -89,23 +90,19 @@
     load.start()
     barrier = pltpu.get_barrier_semaphore()
 
-    @pl.loop(1, groups, unroll=7)
-    def _(k):
-        pl.semaphore_signal(
-            barrier,
-            inc=1,
-            device_id={"grp": lax.rem(group + k, groups)},
-            device_id_type=pl.DeviceIdType.MESH,
-        )
-
-    @pl.loop(1, members)
-    def _(k):
-        pl.semaphore_signal(
-            barrier,
-            inc=1,
-            device_id={"sta": lax.rem(mine + k, members)},
-            device_id_type=pl.DeviceIdType.MESH,
-        )
+    inner = min(INNER, groups)
+    outer = groups // inner
+    line, place = group // inner, lax.rem(group, inner)
+
+    def greet(peer):
+        pl.semaphore_signal(barrier, inc=1, device_id=peer, device_id_type=pl.DeviceIdType.MESH)
+
+    for k in range(1, outer):
+        greet({"grp": lax.rem(line + k, outer) * inner + place})
+    for k in range(1, inner):
+        greet({"grp": line * inner + lax.rem(place + k, inner)})
+    for k in range(1, members):
+        greet({"sta": lax.rem(mine + k, members)})
 
     @pl.loop(0, SEG // STEP)
     def _(step):
@@ -135,7 +132,9 @@
     valid_right = exact_dot_t(pick.astype(jnp.float32), valid)
     owners = owners_ref[...]
     blocks = owners.shape[1]
-    owned = (ints((groups, blocks), 0) == owners).astype(jnp.float32)
+    named = ints((groups, blocks), 0)
+    named = lax.rem(named, outer) * inner + named // outer
+    owned = (named == owners).astype(jnp.float32)
     earlier = (ints((blocks, blocks), 0) < ints((blocks, blocks), 1)).astype(jnp.float32)
     rank = exact_dot(owned, earlier)
     ontos = []
@@ -199,7 +198,7 @@
             )
         return copies
 
-    pl.semaphore_wait(barrier, members - 1 + groups - 1)
+    pl.semaphore_wait(barrier, members - 1 + inner - 1 + outer - 1)
     for k in range(1, members):
         for copy in near(k):
             copy.start()
@@ -233,30 +232,44 @@
             for chunk in range(NB // 128):
                 row = slot * (2 * NB // 128) + part * (NB // 128) + chunk
                 staged[:, row, :] = placed[:, chunk * 128 : (chunk + 1) * 128]
-    routed[...] = staged[...].astype(jnp.bfloat16)
-
-    def far(k):
-        peer = lax.rem(group + k, groups)
+    routed[...] = staged[...].astype(jnp.bfloat16).reshape(routed.shape)
+
+    def along(k):
+        peer = lax.rem(place + k, inner)
         return pltpu.make_async_remote_copy(
             src_ref=routed.at[peer],
-            dst_ref=arrived.at[group],
+            dst_ref=passing.at[place],
             send_sem=far_send.at[k],
             recv_sem=far_recv.at[k],
-            device_id={"grp": peer},
+            device_id={"grp": line * inner + peer},
             device_id_type=pl.DeviceIdType.MESH,
         )
 
-    @pl.loop(1, groups, unroll=7)
-    def _(k):
-        far(k).start()
-
-    arrived[group] = routed[group]
-
-    @pl.loop(1, groups, unroll=7)
-    def _(k):
-        far(k).wait()
-
-    out_ref[...] = arrived[...]
+    def across(k):
+        peer = lax.rem(line + k, outer)
+        return pltpu.make_async_remote_copy(
+            src_ref=passing.at[:, peer],
+            dst_ref=arrived.at[line],
+            send_sem=far_send.at[inner + k],
+            recv_sem=far_recv.at[inner + k],
+            device_id={"grp": peer * inner + place},
+            device_id_type=pl.DeviceIdType.MESH,
+        )
+
+    order = sorted(range(1, inner), key=lambda k: -min(k, inner - k))
+    for k in order:
+        along(k).start()
+    passing[place] = routed[place]
+    for k in order:
+        along(k).wait()
+    order = sorted(range(1, outer), key=lambda k: -min(k, outer - k))
+    for k in order:
+        across(k).start()
+    arrived[line] = passing[:, line]
+    for k in order:
+        across(k).wait()
+
+    out_ref[...] = arrived[...].reshape(out_ref.shape)
 
 
 def to_lags(arrived_ref, coarse_ref, fine_ref, out_ref, staged):
@@ -305,6 +318,8 @@
 
     vmem = pl.BlockSpec(memory_space=pltpu.VMEM)
     tile = (groups, CAP * 2 * NB // 128, 128)
+    inner = min(INNER, groups)
+    outer = groups // inner
     arrived = pl.pallas_call(
         functools.partial(combine, members, groups, stations, windows, phases),
         out_shape=jax.ShapeDtypeStruct(tile, jnp.bfloat16),
@@ -321,13 +336,14 @@
             pltpu.VMEM((combos, 2 * NB), jnp.float32),
             pltpu.VMEM((members * SPLIT, windows), jnp.float32),
             pltpu.VMEM(tile, jnp.float32),
-            pltpu.VMEM(tile, jnp.bfloat16),
-            pltpu.VMEM(tile, jnp.bfloat16),
+            pltpu.VMEM((inner, outer) + tile[1:], jnp.bfloat16),
+            pltpu.VMEM((inner, outer) + tile[1:], jnp.bfloat16),
+            pltpu.VMEM((outer, inner) + tile[1:], jnp.bfloat16),
             pltpu.SemaphoreType.DMA,
             pltpu.SemaphoreType.DMA((members, SPLIT + 1)),
             pltpu.SemaphoreType.DMA((members, SPLIT + 1)),
-            pltpu.SemaphoreType.DMA((groups,)),
-            pltpu.SemaphoreType.DMA((groups,)),
+            pltpu.SemaphoreType.DMA((inner + outer,)),
+            pltpu.SemaphoreType.DMA((inner + outer,)),
         ],
         compiler_params=pltpu.CompilerParams(collective_id=0, has_side_effects=True),
         name="combine",

time: 44.9 us -> 45 us (level)
  no operation moved by 1% of the time
where the time goes in v5:
time: 45 us; the launch traced here: 44.9 us
  Pallas kernels  44.9 us (100%)
    pallas_call x1, Pallas kernels, local(): pl.pallas_call(functools.partial(combine, members, groups, stations, wind...  41.4 us
    pallas_call x1, Pallas kernels, local(): pl.pallas_call(to_lags, out_shape=jax.ShapeDtypeStruct((groups, CAP, 1, 2...  3.45 us

profile of v5, /device:TPU:1, one launch (start us, length us, event | category | flops | bytes accessed | tf_op | source)
XLA Modules:
  0.0 44.9 jit_solution(15061754012868701194)
XLA Ops:
  0.0 41.4 %combine.1.arrived_ref = bf16[64,8,128]{2,1,0:T(8,128)(2,1)} custom-call(f32[64,4,2063]{2,1,0:T(4,128)} %bitcast.4, f32[4,16]{1,0:T(4,128)} %refs_1_.1, s32[16,32]{1,0:T(8,128)} %bitcast.5, s32[1,72]{1,0:T(1,128)} %bitcast.6, f32[32,512]{1,0:T(8,128)} %constant.15.clone.refs_4_.coarse_ref, f32[64,512]{1,0:T(8,128)} %constant.16.clone.refs_5_.fine_ref, ...), custom_call_target="tpu_custom_call" | custom-call | tf_op jit(solution)/shard_map/combine/pallas_call | solution.py:323
  41.4 3.5 %to_lags.1 = f32[64,2,1,2001]{3,2,1,0:T(1,128)} custom-call(bf16[64,8,128]{2,1,0:T(8,128)(2,1)} %combine.1.arrived_ref, f32[32,512]{1,0:T(8,128)} %constant.15.clone.refs_4_.coarse_ref, f32[64,512]{1,0:T(8,128)} %constant.16.clone.refs_5_.fine_ref), custom_call_target="tpu_custom_call" | custom-call | tf_op jit(solution)/shard_map/to_lags/pallas_call | solution.py:363

commit v6 on v5

--- a/solution.py
+++ b/solution.py
@@ -79,8 +79,9 @@
     (raw_hbm, taps_ref, valid_ref, owners_ref) = refs[:4]
     (coarse_ref, fine_ref, adv_ref, edge_ref, smooth_ref, lead_ref, spread_ref) = refs[4:11]
     out_ref = refs[11]
-    (raw, waves, rest, whole, white, left, right, stack, held, staged, routed) = refs[12:23]
-    passing, arrived, raw_sem, near_send, near_recv, far_send, far_recv = refs[23:]
+    (raw, waves, rest, whole, white, left, right, stack, held, staged) = refs[12:22]
+    (routed_z, passing_z, arrived_y, routed_y, passing_y, arrived_z) = refs[22:28]
+    raw_sem, near_send, near_recv, far_send, far_recv = refs[28:]
     mine = lax.axis_index("sta")
     group = lax.axis_index("grp")
     half = stations // SPLIT
@@ -132,13 +133,14 @@
     valid_right = exact_dot_t(pick.astype(jnp.float32), valid)
     owners = owners_ref[...]
     blocks = owners.shape[1]
-    named = ints((groups, blocks), 0)
-    named = lax.rem(named, outer) * inner + named // outer
-    owned = (named == owners).astype(jnp.float32)
     earlier = (ints((blocks, blocks), 0) < ints((blocks, blocks), 1)).astype(jnp.float32)
-    rank = exact_dot(owned, earlier)
     ontos = []
     for slot in range(CAP):
+        named = ints((groups, blocks), 0)
+        if slot == 0:
+            named = lax.rem(named, outer) * inner + named // outer
+        owned = (named == owners).astype(jnp.float32)
+        rank = exact_dot(owned, earlier)
         chosen = jnp.where(jnp.abs(rank - slot) < 0.5, owned, 0.0)
         onto = jnp.dot(
             chosen.astype(jnp.bfloat16), spread_ref[...], preferred_element_type=jnp.float32
@@ -230,46 +232,54 @@
         for part, moved in enumerate((moved_re, moved_im)):
             placed = jnp.dot(ontos[slot], moved, preferred_element_type=jnp.float32)
             for chunk in range(NB // 128):
-                row = slot * (2 * NB // 128) + part * (NB // 128) + chunk
-                staged[:, row, :] = placed[:, chunk * 128 : (chunk + 1) * 128]
-    routed[...] = staged[...].astype(jnp.bfloat16).reshape(routed.shape)
-
-    def along(k):
+                row = part * (NB // 128) + chunk
+                staged[slot, :, row, :] = placed[:, chunk * 128 : (chunk + 1) * 128]
+    for slot, side in enumerate((routed_z, routed_y)):
+        side[...] = staged[slot].astype(jnp.bfloat16).reshape(side.shape)
+
+    def along_z(k, src, dst, first):
         peer = lax.rem(place + k, inner)
         return pltpu.make_async_remote_copy(
-            src_ref=routed.at[peer],
-            dst_ref=passing.at[place],
-            send_sem=far_send.at[k],
-            recv_sem=far_recv.at[k],
+            src_ref=src.at[peer] if first else src.at[:, peer],
+            dst_ref=dst.at[place],
+            send_sem=far_send.at[1 - first, k],
+            recv_sem=far_recv.at[1 - first, k],
             device_id={"grp": line * inner + peer},
             device_id_type=pl.DeviceIdType.MESH,
         )
 
-    def across(k):
+    def along_y(k, src, dst, first):
         peer = lax.rem(line + k, outer)
         return pltpu.make_async_remote_copy(
-            src_ref=passing.at[:, peer],
-            dst_ref=arrived.at[line],
-            send_sem=far_send.at[inner + k],
-            recv_sem=far_recv.at[inner + k],
+            src_ref=src.at[peer] if first else src.at[:, peer],
+            dst_ref=dst.at[line],
+            send_sem=far_send.at[1 - first, inner + k],
+            recv_sem=far_recv.at[1 - first, inner + k],
             device_id={"grp": peer * inner + place},
             device_id_type=pl.DeviceIdType.MESH,
         )
 
-    order = sorted(range(1, inner), key=lambda k: -min(k, inner - k))
-    for k in order:
-        along(k).start()
-    passing[place] = routed[place]
-    for k in order:
-        along(k).wait()
-    order = sorted(range(1, outer), key=lambda k: -min(k, outer - k))
-    for k in order:
-        across(k).start()
-    arrived[line] = passing[:, line]
-    for k in order:
-        across(k).wait()
-
-    out_ref[...] = arrived[...].reshape(out_ref.shape)
+    far_z = sorted(range(1, inner), key=lambda k: -min(k, inner - k))
+    far_y = sorted(range(1, outer), key=lambda k: -min(k, outer - k))
+    copies = [along_z(k, routed_z, passing_z, 1) for k in far_z]
+    copies += [along_y(k, routed_y, passing_y, 1) for k in far_y]
+    for copy in copies:
+        copy.start()
+    passing_z[place] = routed_z[place]
+    passing_y[line] = routed_y[line]
+    for copy in copies:
+        copy.wait()
+    copies = [along_y(k, passing_z, arrived_y, 0) for k in far_y]
+    copies += [along_z(k, passing_y, arrived_z, 0) for k in far_z]
+    for copy in copies:
+        copy.start()
+    arrived_y[line] = passing_z[:, line]
+    arrived_z[place] = passing_y[:, place]
+    for copy in copies:
+        copy.wait()
+    for n in range(outer):
+        out_ref[0, n * inner : (n + 1) * inner] = arrived_y[n]
+        out_ref[1, n * inner : (n + 1) * inner] = arrived_z[:, n]
 
 
 def to_lags(arrived_ref, coarse_ref, fine_ref, out_ref, staged):
@@ -277,10 +287,10 @@
     chunks = 2 * NB // 128
     sides = []
     for slot in range(CAP):
-        parts = [staged[:, slot * chunks + c, :] for c in range(chunks)]
+        parts = [staged[slot, :, c, :] for c in range(chunks)]
         sides.append(jnp.concatenate(parts, axis=1))
     stacks = jnp.concatenate(sides, axis=0).astype(jnp.bfloat16)
-    groups = arrived_ref.shape[0]
+    groups = arrived_ref.shape[1]
     fr, fi = fine_ref[:, :NB], fine_ref[:, NB:]
     lags = out_ref.shape[-1]
     wide = 2 * STEP
@@ -317,7 +327,7 @@
     spread = jnp.asarray(pair_spread(members), jnp.bfloat16)
 
     vmem = pl.BlockSpec(memory_space=pltpu.VMEM)
-    tile = (groups, CAP * 2 * NB // 128, 128)
+    tile = (CAP, groups, 2 * NB // 128, 128)
     inner = min(INNER, groups)
     outer = groups // inner
     arrived = pl.pallas_call(
@@ -336,14 +346,17 @@
             pltpu.VMEM((combos, 2 * NB), jnp.float32),
             pltpu.VMEM((members * SPLIT, windows), jnp.float32),
             pltpu.VMEM(tile, jnp.float32),
-            pltpu.VMEM((inner, outer) + tile[1:], jnp.bfloat16),
-            pltpu.VMEM((inner, outer) + tile[1:], jnp.bfloat16),
-            pltpu.VMEM((outer, inner) + tile[1:], jnp.bfloat16),
+            pltpu.VMEM((inner, outer) + tile[2:], jnp.bfloat16),
+            pltpu.VMEM((inner, outer) + tile[2:], jnp.bfloat16),
+            pltpu.VMEM((outer, inner) + tile[2:], jnp.bfloat16),
+            pltpu.VMEM((outer, inner) + tile[2:], jnp.bfloat16),
+            pltpu.VMEM((outer, inner) + tile[2:], jnp.bfloat16),
+            pltpu.VMEM((inner, outer) + tile[2:], jnp.bfloat16),
             pltpu.SemaphoreType.DMA,
             pltpu.SemaphoreType.DMA((members, SPLIT + 1)),
             pltpu.SemaphoreType.DMA((members, SPLIT + 1)),
-            pltpu.SemaphoreType.DMA((inner + outer,)),
-            pltpu.SemaphoreType.DMA((inner + outer,)),
+            pltpu.SemaphoreType.DMA((2, inner + outer)),
+            pltpu.SemaphoreType.DMA((2, inner + outer)),
         ],
         compiler_params=pltpu.CompilerParams(collective_id=0, has_side_effects=True),
         name="combine",

time: 45 us -> 44 us (0.978)
  Pallas kernels: 44.9 us -> 43.8 us
    pallas_call x1, Pallas kernels: 41.4 us -> 40.4 us  [local(): pl.pallas_call(functools.partial(combine, members, groups, stations, wind...]
where the time goes in v6:
time: 44 us; the launch traced here: 43.8 us
  Pallas kernels  43.8 us (100%)
    pallas_call x1, Pallas kernels, local(): pl.pallas_call(functools.partial(combine, members, groups, stations, wind...  40.4 us
    pallas_call x1, Pallas kernels, local(): pl.pallas_call(to_lags, out_shape=jax.ShapeDtypeStruct((groups, CAP, 1, 2...  3.48 us

profile of v6, /device:TPU:1, one launch (start us, length us, event | category | flops | bytes accessed | tf_op | source)
XLA Modules:
  0.0 43.8 jit_solution(10533598155007030941)
XLA Ops:
  0.0 40.4 %combine.1.arrived_ref = bf16[2,64,4,128]{3,2,1,0:T(4,128)(2,1)} custom-call(f32[64,4,2063]{2,1,0:T(4,128)} %bitcast.4, f32[4,16]{1,0:T(4,128)} %refs_1_.1, s32[16,32]{1,0:T(8,128)} %bitcast.5, s32[1,72]{1,0:T(1,128)} %bitcast.6, f32[32,512]{1,0:T(8,128)} %constant.15.clone.refs_4_.coarse_ref, f32[64,512]{1,0:T(8,128)} %constant.16.clone.refs_5_.fine_ref, ...), custom_call_target="tpu_custom_call" | custom-call | tf_op jit(solution)/shard_map/combine/pallas_call | solution.py:333
  40.4 3.5 %to_lags.1 = f32[64,2,1,2001]{3,2,1,0:T(1,128)} custom-call(bf16[2,64,4,128]{3,2,1,0:T(4,128)(2,1)} %combine.1.arrived_ref, f32[32,512]{1,0:T(8,128)} %constant.15.clone.refs_4_.coarse_ref, f32[64,512]{1,0:T(8,128)} %constant.16.clone.refs_5_.fine_ref), custom_call_target="tpu_custom_call" | custom-call | tf_op jit(solution)/shard_map/to_lags/pallas_call | solution.py:376
